TPU v7x, 512 devices: a whole 4x8x8 slice. The times are simulated.
512 devices in a mesh: axial: 32 (over x, z), pitch: 8 (over y_lo, core), span: 2 (over y_hi).
Axes of the slice: x: 4, y: 8 (y_hi: 2, y_lo: 4; y = y_hi * 4 + y_lo), z: 8, core: 2. Of those that a mesh axis runs over, the one named last changes fastest.
Arguments:
- flow_state: float32 [5, 512, 64, 1024], P(None, 'axial', 'pitch', 'span')
- step_start: float32 [5, 512, 64, 1024], P(None, 'axial', 'pitch', 'span')
- lower_coef: float32 [16, 5, 512, 1024], P('pitch', None, 'axial', 'span')
- upper_coef: float32 [16, 5, 512, 1024], P('pitch', None, 'axial', 'span')
- partner_row: int32 [2, 512], P(None, 'axial'), may hold values from 0 to 511, as said below
- periodic_cells: int32 [2, 512], P(None, 'axial'), may hold values from 1 to 1024, as said below
- phase_angles: float32 [2], replicated, may hold values from -3.140625 to 3.140625
Outputs:
- next_state: float32 [5, 512, 64, 1024], P(None, 'axial', 'pitch', 'span')
Inputs may be any that keep to these rules, and one draw needn't show every extreme that they name: `partner_row`: each row is a permutation of 0 .. 511 and row 1 is the inverse of row 0. Of the 16 rows of one axial device, in either row, exactly 1 name rows of each of 16 devices and none of any other device. `periodic_cells`: rows 128 up to 384 have 1 to 128 periodic cells; all other rows have 1024.
All inputs are finite; a program needn't handle non-finite values.
Results may differ from a plain program's by a relative error of at most 0.00005.
Values sent between devices are 32-bit elements; how exact they have to be, the bound alone decides.
A program may use at most 64 MiB of HBM per device.

v0:
```python
import jax
import jax.numpy as jnp
from jax import lax
from jax.sharding import PartitionSpec as P

DISSIPATION = 0.25
SECTION_STEP = 0.5
MIRROR = (1.0, 1.0, -1.0, 1.0, 1.0)


def grouped_exchange(shard, axis, split_dim, concat_dim, work, item_dim, out_dim):

    def moved(group):
        return lax.all_to_all(group, axis, split_axis=split_dim, concat_axis=concat_dim, tiled=True)

    items = jax.tree.leaves(shard)[0].shape[item_dim]
    ends = [items * k // 2 for k in range(2 + 1)] if items % 2 == 0 else [0, items]
    groups = [
        jax.tree.map(lambda a: lax.slice_in_dim(a, low, high, axis=item_dim), shard)
        for low, high in zip(ends, ends[1:])
    ]
    arrived = [moved(group) for group in groups]
    made = [work(group) for group in arrived]
    return jax.tree.map(lambda *parts: jnp.concatenate(parts, axis=out_dim), *made)


def filled_up(lines, count):
    spare = -lines.shape[0] % count
    if not spare:
        return lines
    return jnp.concatenate([lines, jnp.zeros((spare, *lines.shape[1:]), lines.dtype)])


def sum_by_parts(shard, axis):
    lines = shard.reshape(-1, *shard.shape[1:][-1:])
    padded = filled_up(lines, lax.axis_size(axis))
    own = lax.psum_scatter(padded, axis, scatter_dimension=0, tiled=True)
    whole = lax.all_gather(own, axis, axis=0, tiled=True)
    return whole[: len(lines)].reshape(shard.shape)


def extended(block, sides, width, periodic):
    for axis, dim in sides:
        count = lax.axis_size(axis)
        forward = [(i, i + 1) for i in range(count - 1)]
        if periodic:
            forward.append((count - 1, 0))
        backward = [(target, source) for source, target in forward]
        low = lax.ppermute(
            lax.slice_in_dim(block, block.shape[dim] - width, None, axis=dim), axis, forward
        )
        high = lax.ppermute(lax.slice_in_dim(block, 0, width, axis=dim), axis, backward)
        block = jnp.concatenate([low, block, high], axis=dim)
    return block


def euler_flux(fields, direction):
    density = fields[0]
    velocity = fields[direction] / density
    pressure = 0.4 * (
        fields[4]
        - 0.5 * (fields[1] * fields[1] + fields[2] * fields[2] + fields[3] * fields[3]) / density
    )
    components = [
        fields[direction],
        fields[1] * velocity,
        fields[2] * velocity,
        fields[3] * velocity,
        (fields[4] + pressure) * velocity,
    ]
    components[direction] = components[direction] + pressure
    return jnp.stack(components)


def section_update(center, start_state, lows, highs):
    residual_sum = jnp.zeros_like(center)
    for direction in range(3):
        lower_side = lows[direction]
        upper_side = highs[direction]
        residual_sum = (
            residual_sum
            - 0.5 * (euler_flux(upper_side, direction + 1) - euler_flux(lower_side, direction + 1))
            + DISSIPATION * (upper_side + lower_side - 2.0 * center)
        )
    return start_state + SECTION_STEP * residual_sum


def term_basis(phase_value, term_ids):
    harmonic = ((term_ids + 1) // 2).astype(phase_value.dtype)
    return jnp.where(
        (term_ids % 2 == 0) & (term_ids > 0),
        jnp.sin(harmonic * phase_value),
        jnp.cos(harmonic * phase_value),
    )


def per_device(
    flow_state, step_start, lower_coef, upper_coef, partner_row, periodic_cells, phase_angles
):
    n_axial = lax.axis_size("axial")
    n_pitch = lax.axis_size("pitch")
    n_span = lax.axis_size("span")
    axial_at = lax.axis_index("axial")
    pitch_at = lax.axis_index("pitch")
    span_at = lax.axis_index("span")
    var_count, ax_cells, pi_cells, sp_cells = flow_state.shape
    term_count = lower_coef.shape[0]
    capacity = max(1, ax_cells // n_axial)
    term_ids = pitch_at * term_count + jnp.arange(term_count, dtype=jnp.int32)
    basis_pair = jnp.stack(
        [term_basis(phase_angles[1], term_ids), term_basis(phase_angles[0], term_ids)]
    )
    coef_pair = jnp.stack([lower_coef, upper_coef])
    device_ids = jnp.arange(n_axial, dtype=jnp.int32)
    slot_ids = jnp.arange(capacity, dtype=jnp.int32)
    local_order = jnp.arange(ax_cells, dtype=jnp.int32)
    target_dev = partner_row // ax_cells
    partner_local = partner_row % ax_cells
    same_target = target_dev[:, None, :] == target_dev[:, :, None]
    earlier = same_target & (local_order[None, None, :] < local_order[None, :, None])
    send_rank = jnp.sum(earlier.astype(jnp.int32), axis=2)
    send_table = (
        (target_dev[:, None, None, :] == device_ids[None, :, None, None])
        & (send_rank[:, None, None, :] == slot_ids[None, None, :, None])
    ).astype(jnp.float32)
    before = same_target & (partner_local[:, None, :] < partner_local[:, :, None])
    recv_rank = jnp.sum(before.astype(jnp.int32), axis=2)
    recv_table = (
        (target_dev[:, :, None, None] == device_ids[None, None, :, None])
        & (recv_rank[:, :, None, None] == slot_ids[None, None, None, :])
    ).astype(jnp.float32)
    packed = jnp.einsum(
        "fncr,ftvrs->nfctvs", send_table, coef_pair, precision=lax.Precision.HIGHEST
    )

    def evaluate(slot_block):
        return jnp.einsum(
            "ft,nfktvs->nfkvs", basis_pair, slot_block, precision=lax.Precision.HIGHEST
        )

    received = grouped_exchange(packed, "axial", 0, 0, evaluate, 2, 2)
    ghost_part = jnp.einsum(
        "grac,agcvs->gvrs", recv_table, received[:, ::-1], precision=lax.Precision.HIGHEST
    )
    ghost_pair = sum_by_parts(ghost_part, "pitch")
    padded = extended(flow_state, (("axial", 1), ("pitch", 2)), 1, False)
    spanned = extended(flow_state, (("span", 3),), 1, True)
    span_pos = span_at * sp_cells + jnp.arange(sp_cells, dtype=jnp.int32)
    total_span = sp_cells * n_span
    open_rows = span_pos[None, None, :] >= total_span - periodic_cells[:, :, None]
    mirror_sign = jnp.array(MIRROR, jnp.float32)[None, :, None, None]
    face_cells = (
        jnp.stack([flow_state[:, :, 0, :], flow_state[:, :, pi_cells - 1, :]]) * mirror_sign
    )
    ghost_rows = jnp.where(open_rows[:, None], ghost_pair, face_cells)
    row_ids = jnp.arange(ax_cells, dtype=jnp.int32)[None, :, None, None]
    axial_low = jnp.where((axial_at == 0) & (row_ids == 0), flow_state, padded[:, :-2, 1:-1])
    axial_high = jnp.where(
        (axial_at == n_axial - 1) & (row_ids == ax_cells - 1), flow_state, padded[:, 2:, 1:-1]
    )
    col_ids = jnp.arange(pi_cells, dtype=jnp.int32)[None, None, :, None]
    pitch_low = jnp.where(
        (pitch_at == 0) & (col_ids == 0), ghost_rows[0][:, :, None, :], padded[:, 1:-1, :-2]
    )
    pitch_high = jnp.where(
        (pitch_at == n_pitch - 1) & (col_ids == pi_cells - 1),
        ghost_rows[1][:, :, None, :],
        padded[:, 1:-1, 2:],
    )
    span_low = spanned[..., :-2]
    span_high = spanned[..., 2:]
    return section_update(
        flow_state,
        step_start,
        (axial_low, pitch_low, span_low),
        (axial_high, pitch_high, span_high),
    )


def solution(mesh):
    in_specs = (
        P(None, "axial", "pitch", "span"),
        P(None, "axial", "pitch", "span"),
        P("pitch", None, "axial", "span"),
        P("pitch", None, "axial", "span"),
        P(None, "axial"),
        P(None, "axial"),
        P(),
    )
    out_specs = P(None, "axial", "pitch", "span")
    return jax.shard_map(
        per_device, mesh=mesh, in_specs=in_specs, out_specs=out_specs, check_vma=False
    )
```

profile of v0, /device:TPU:1, one launch (start us, length us, event | category | flops | bytes accessed | tf_op | source)
XLA Modules:
  0.0 147.3 jit_solution(15030729927473571792)
XLA Ops:
  0.0 0.7 and_select_fusion
  0.7 0.2 convert_reduce_fusion
  0.9 1.9 %convolution_bitcast_fusion = f32[32,2,1,2,5,512]{5,0,4,3,1,2:T(8,128)S(1)} fusion(f32[1,2,5,16,512]{4,3,2,1,0:T(8,128)} %bitcast.53, f32[1,2,5,16,512]{4,3,2,1,0:T(8,128)} %bitcast.54, s32[2,16]{1,0:T(2,128)S(1)} %get-tuple-element.51, pred[2,16]{1,0:T(4,128)(4,1)S(1)} %get-tuple-element.57), kind=kOutput, calls=%fused_computation | convolution fusion | flops 63080448 | bytes 1966240 | tf_op jit(solution)/shard_map/fncr,ftvrs->nfctvs/dot_general | solution.py:132
  2.8 2.1 %copy.55 = f32[32,2,1,2,5,512]{5,3,4,2,1,0:T(2,128)} copy(f32[32,2,1,2,5,512]{5,0,4,3,1,2:T(8,128)S(1)} %convolution_bitcast_fusion) | data formatting | bytes 2621440 | tf_op jit(solution)/shard_map/fncr,ftvrs->nfctvs/transpose | solution.py:132
  4.9 13.8 %all-to-all-start = ((f32[32,2,1,2,5,512]{5,3,4,2,1,0:T(2,128)}), f32[32,2,1,2,5,512]{5,3,4,2,1,0:T(2,128)}, u32[]{:S(2)}, u32[]{:S(2)}) async-start(f32[32,2,1,2,5,512]{5,3,4,2,1,0:T(2,128)} %copy.55), calls=%async_computation | async-start | bytes 2621440 | tf_op jit(solution)/shard_map/all_to_all | solution.py:14
  18.7 1.6 %fusion.35 = (f32[5,1,8,512]{3,2,1,0:T(8,128)S(1)}, f32[5,1,8,512]{3,2,1,0:T(8,128)}) fusion(f32[5,16,8,512]{3,2,1,0:T(8,128)} %param.8), kind=kLoop, calls=%fused_computation.136 | loop fusion | bytes 327680 | tf_op jit(solution)/shard_map/slice | solution.py:50
  20.3 1.3 collective-permute-start
  21.6 4.6 %collective-permute-start.1 = (f32[5,1,8,512]{3,2,1,0:T(8,128)S(1)}, f32[5,1,8,512]{3,2,1,0:T(8,128)}, u32[]{:S(2)}, u32[]{:S(2)}) collective-permute-start(f32[5,1,8,512]{3,2,1,0:T(8,128)S(1)} %get-tuple-element.42), channel_id=1, source_target_pairs={{0,16},{16,32},{32,48},{48,64},{64,80},{80,96},{96,112},{112,128},... | collective-permute-start | bytes 245768 | tf_op jit(solution)/shard_map/ppermute | solution.py:49
  26.2 2.1 %constant_dynamic-update-slice_fusion.1 = (f32[5,16,8,513]{3,1,2,0:T(8,128)S(1)}, f32[5,16,8,512]{3,1,2,0:T(8,128)S(1)}) fusion(f32[5,16,8,512]{3,2,1,0:T(8,128)} %param.8), kind=kLoop, calls=%fused_computation.87 | loop fusion | bytes 3932160
  28.3 0.9 fusion.36
  29.3 7.4 %collective-permute-start.5 = (f32[5,16,8,1]{3,1,2,0:T(8,128)}, f32[5,16,8,1]{3,1,2,0:T(8,128)S(1)}, u32[]{:S(2)}, u32[]{:S(2)}) collective-permute-start(f32[5,16,8,1]{3,1,2,0:T(8,128)} %get-tuple-element.45), channel_id=1, source_target_pairs={{0,1},{1,0},{2,3},{3,2},{4,5},{5,4},{6,7},{7,6},{8,9},{9,8},{10,11... | collective-permute-start | bytes 7688 | tf_op jit(solution)/shard_map/ppermute | solution.py:49
  36.7 1.9 %collective-permute-start.4 = (f32[5,16,8,1]{3,1,2,0:T(8,128)}, f32[5,16,8,1]{3,1,2,0:T(8,128)}, u32[]{:S(2)}, u32[]{:S(2)}) collective-permute-start(f32[5,16,8,1]{3,1,2,0:T(8,128)} %get-tuple-element.44), channel_id=1, source_target_pairs={{1,0},{0,1},{3,2},{2,3},{5,4},{4,5},{7,6},{6,7},{9,8},{8,9},{11,10... | collective-permute-start | bytes 7688 | tf_op jit(solution)/shard_map/ppermute | solution.py:52
  38.6 2.8 %fusion.34 = (f32[5,16,1,512]{3,2,1,0:T(1,128)S(1)}, f32[5,16,1,512]{3,2,1,0:T(1,128)}) fusion(f32[5,16,8,512]{3,2,1,0:T(8,128)} %param.8), kind=kLoop, calls=%fused_computation.135 | loop fusion | bytes 655360 | tf_op jit(solution)/shard_map/slice | solution.py:153
  41.4 0.6 fusion.37
  42.0 1.3 cosine_select_fusion
  43.4 1.7 %copy_bitcast_fusion.1 = (f32[1,5,16,512]{3,2,1,0:T(8,128)}, f32[1,5,16,512]{3,2,1,0:T(8,128)}) fusion(f32[5,16,1,512]{3,2,1,0:T(1,128)} %get-tuple-element.41, f32[5,16,1,512]{3,2,1,0:T(1,128)S(1)} %get-tuple-element.40), kind=kLoop, calls=%fused_computation.84 | loop fusion | bytes 655360 | tf_op jit(solution)/shard_map/stack;squeeze | solution.py:153
  45.0 0.7 broadcast_compare_fusion
  45.7 0.6 compare_and_fusion.2
  46.3 0.6 compare_and_fusion.5
  46.9 1.3 dynamic-slice.4
  48.9 7.5 %collective-permute-done.4 = f32[5,16,8,1]{3,1,2,0:T(8,128)} collective-permute-done((f32[5,16,8,1]{3,1,2,0:T(8,128)}, f32[5,16,8,1]{3,1,2,0:T(8,128)}, u32[]{:S(2)}, u32[]{:S(2)}) %collective-permute-start.4) | collective-permute-done | bytes 2592 | tf_op jit(solution)/shard_map/ppermute | solution.py:52
  56.3 1.0 constant_dynamic-update-slice_fusion
  57.3 0.1 constant_dynamic-update-slice_fusion.2
  57.5 0.1 slice_dynamic-update-slice_fusion
  57.6 0.3 multiply_dynamic-update-slice_fusion.5
  57.9 0.1 multiply_dynamic-update-slice_fusion.4
  58.0 0.4 add_dynamic-update-slice_fusion.1
  58.4 0.2 multiply_dynamic-update-slice_fusion.2
  58.7 0.1 multiply_dynamic-update-slice_fusion.1
  58.8 0.2 add_dynamic-update-slice_fusion
  59.0 0.1 multiply_dynamic-update-slice_fusion
  59.1 0.1 multiply_dynamic-update-slice_fusion.3
  59.3 0.9 copy-done
  60.2 1.1 copy-done.2
  61.3 1.0 copy.49
  62.3 1.0 copy.51
  63.2 5.9 %fusion.14 = f32[2,1,32,5,512]{4,1,3,2,0:T(1,128)S(1)} fusion(f32[2,2,1,1,1]{1,2,4,3,0:T(1,128)S(1)} %bitcast.55, f32[32,2,1,2,5,512]{5,3,4,2,1,0:T(2,128)} %all-to-all-done), kind=kOutput, calls=%fused_computation.24 | convolution fusion | flops 3932160 | bytes 1966096 | tf_op jit(solution)/shard_map/ft,nfktvs->nfkvs/dot_general | solution.py:137
  69.2 0.9 copy.82
  70.1 2.0 %rev.3 = f32[32,2,1,5,512]{4,0,3,1,2:T(8,128)} reverse(f32[32,2,1,5,512]{4,0,3,1,2:T(8,128)} %bitcast.51), dimensions={1} | reverse | bytes 1310720 | tf_op jit(solution)/shard_map/rev | solution.py:143
  72.1 2.2 %fusion.19 = f32[2,5,512,16]{2,3,1,0:T(8,128)} fusion(f32[32,2,1,5,512]{4,0,3,1,2:T(8,128)} %rev.3, s32[2,16]{1,0:T(2,128)S(1)} %get-tuple-element.51, pred[2,16]{1,0:T(4,128)(4,1)S(1)} %get-tuple-element.56), kind=kOutput, calls=%fused_computation.29 | convolution fusion | flops 31459328 | bytes 983200 | tf_op jit(solution)/shard_map/grac,agcvs->gvrs/dot_general | solution.py:142
  74.2 25.7 %fusion = f32[24,512]{1,0:T(8,128)S(1)} fusion(f32[160,512]{1,0:T(8,128)} %bitcast.52), kind=kCustom, calls=%all-reduce-scatter | all-reduce-scatter fusion | flops 98305 | bytes 378880
  99.9 3.1 %collective-permute-start.6 = (f32[24,512]{1,0:T(8,128)S(1)}, f32[24,512]{1,0:T(8,128)}, u32[]{:S(2)}, u32[]{:S(2)}) collective-permute-start(f32[24,512]{1,0:T(8,128)S(1)} %fusion), channel_id=1, source_target_pairs={{0,2},{2,4},{4,6},{6,8},{8,10},{10,12},{12,14},{1,3},{3,5},{5,7},{... | collective-permute-start | bytes 147464
  103.1 1.7 %collective-permute-start.7 = (f32[4,512]{1,0:T(4,128)S(1)}, f32[4,512]{1,0:T(4,128)S(1)}, u32[]{:S(2)}, u32[]{:S(2)}) collective-permute-start(f32[4,512]{1,0:T(4,128)S(1)} %slice.292), channel_id=1, source_target_pairs={{0,4},{2,6},{4,8},{6,10},{8,12},{10,14},{1,5},{3,7},{5,9},{7,11},{... | collective-permute-start | bytes 24584
  104.8 0.9 pad_maximum_fusion.14
  105.7 4.5 %collective-permute-start.2 = (f32[5,18,1,512]{3,1,2,0:T(8,128)}, f32[5,18,1,512]{3,1,2,0:T(8,128)}, u32[]{:S(2)}, u32[]{:S(2)}) collective-permute-start(f32[5,18,1,512]{3,1,2,0:T(8,128)} %get-tuple-element.37), channel_id=1, source_target_pairs={{2,0},{4,2},{6,4},{8,6},{10,8},{12,10},{14,12},{3,1},{5,3},{7,5},{... | collective-permute-start | bytes 552968 | tf_op jit(solution)/shard_map/ppermute | solution.py:52
  110.2 1.9 %collective-permute-start.3 = (f32[5,18,1,512]{3,1,2,0:T(8,128)}, f32[5,18,1,512]{3,1,2,0:T(8,128)}, u32[]{:S(2)}, u32[]{:S(2)}) collective-permute-start(f32[5,18,1,512]{3,1,2,0:T(8,128)} %get-tuple-element.36), channel_id=1, source_target_pairs={{0,2},{2,4},{4,6},{6,8},{8,10},{10,12},{12,14},{1,3},{3,5},{5,7},{... | collective-permute-start | bytes 552968 | tf_op jit(solution)/shard_map/ppermute | solution.py:49
  112.1 0.6 copy-done.6
  112.7 2.4 %concatenate.30 = f32[52,512]{1,0:T(8,128)S(1)} concatenate(f32[4,512]{1,0:T(4,128)} %copy-done.6, f32[24,512]{1,0:T(8,128)} %collective-permute-done.6, f32[24,512]{1,0:T(8,128)} %copy-done.5), dimensions={0} | concatenate | bytes 212992
  115.2 16.5 %all-gather = f32[8,20,512]{2,1,0:T(8,128)} all-gather(f32[1,20,512]{2,1,0:T(8,128)S(1)} %dynamic-slice_bitcast_fusion), channel_id=1, replica_groups=mesh['axial'=32,'pitch'=8,'span'=2] {'pitch'}, dimensions={0}, use_global_device_ids=true | all-gather | bytes 368640 | tf_op jit(solution)/shard_map/all_gather | solution.py:38
  131.7 1.8 %reshape.225 = f32[2,5,16,512]{3,2,1,0:T(8,128)} reshape(f32[8,20,512]{2,1,0:T(8,128)} %all-gather) | data formatting | bytes 655360 | tf_op jit(solution)/shard_map/reshape | solution.py:39
  133.5 1.2 fusion.21
  134.8 2.0 %fusion.7 = (f32[5,16,8,512]{3,1,2,0:T(8,128)S(1)}, f32[5,16,8,512]{3,1,2,0:T(8,128)S(1)}, f32[5,16,8,512]{3,1,2,0:T(8,128)S(1)}, f32[5,16,8,512]{3,1,2,0:T(8,128)S(1)}) fusion(f32[5,18,1,512]{3,1,2,0:T(8,128)} %collective-permute-done.3, f32[5,1,8,512]{3,1,2,0:T(1,128)S(1)} %copy.49, f32[5,16,8,512]{3,1,2,0:T(8,128)S(1)} %get-tuple-element.47, ...), kind=kLoop, calls=%fused_computation.9 | loop fusion | flops 3932160 | bytes 7413808 | tf_op jit(solution)/shard_map/jit(_where)/select_n | solution.py:162
  136.8 0.2 add_dynamic-update-slice_fusion.4
  137.1 0.2 add_dynamic-update-slice_fusion.5
  137.4 0.1 multiply_dynamic-update-slice_fusion.8
  137.4 0.2 add_dynamic-update-slice_fusion.2
  137.8 0.2 add_dynamic-update-slice_fusion.3
  138.0 0.1 multiply_dynamic-update-slice_fusion.12
  138.2 0.1 multiply_dynamic-update-slice_fusion.9
  138.3 1.0 copy-done.4
  139.3 0.4 copy-done.3
  139.7 0.4 copy-done.1
  140.1 5.4 %fusion.6 = f32[5,16,8,512]{3,1,2,0:T(8,128)S(1)} fusion(f32[5,16,8,512]{3,1,2,0:T(8,128)S(1)} %get-tuple-element.47, f32[5,16,8,1]{3,1,2,0:T(8,128)S(1)} %collective-permute-done.5, f32[5,16,8,513]{3,1,2,0:T(8,128)S(1)} %constant_dynamic-update-slice_fusion, f32[5,16,8,512]{3,2,1,0:T(8,128)S(1)} %copy-done.4, f32[5,16,8,512]{3,1,2,0:T(8,128)S(1)} %copy-done.3, ...), kind=kLoop, calls=%fused_computation.7 | loop fusion | flops 12124160 | bytes 13969968 | tf_op jit(solution)/shard_map/add | solution.py:85
  145.5 1.8 %copy.66 = f32[5,16,8,512]{3,2,1,0:T(8,128)} copy(f32[5,16,8,512]{3,1,2,0:T(8,128)S(1)} %fusion.6) | data formatting | bytes 2621440 | tf_op jit(solution)/shard_map/add | solution.py:85
  (49 shorter events, 0.7 us)
Async XLA Ops:
  4.9 58.3 %all-to-all-start = ((f32[32,2,1,2,5,512]{5,3,4,2,1,0:T(2,128)}), f32[32,2,1,2,5,512]{5,3,4,2,1,0:T(2,128)}, u32[]{:S(2)}, u32[]{:S(2)}) async-start(f32[32,2,1,2,5,512]{5,3,4,2,1,0:T(2,128)} %copy.55), calls=%async_computation | async-start | bytes 2621440 | tf_op jit(solution)/shard_map/all_to_all | solution.py:14
  20.3 39.9 %collective-permute-start = (f32[5,1,8,512]{3,2,1,0:T(8,128)}, f32[5,1,8,512]{3,2,1,0:T(8,128)}, u32[]{:S(2)}, u32[]{:S(2)}) collective-permute-start(f32[5,1,8,512]{3,2,1,0:T(8,128)} %get-tuple-element.43), channel_id=1, source_target_pairs={{16,0},{32,16},{48,32},{64,48},{80,64},{96,80},{112,96},{128,112},... | collective-permute-start | bytes 245768 | tf_op jit(solution)/shard_map/ppermute | solution.py:52
  21.6 40.6 %collective-permute-start.1 = (f32[5,1,8,512]{3,2,1,0:T(8,128)S(1)}, f32[5,1,8,512]{3,2,1,0:T(8,128)}, u32[]{:S(2)}, u32[]{:S(2)}) collective-permute-start(f32[5,1,8,512]{3,2,1,0:T(8,128)S(1)} %get-tuple-element.42), channel_id=1, source_target_pairs={{0,16},{16,32},{32,48},{48,64},{64,80},{80,96},{96,112},{112,128},... | collective-permute-start | bytes 245768 | tf_op jit(solution)/shard_map/ppermute | solution.py:49
  28.3 13.1 %copy-start.11 = (f32[2]{0:T(128)S(1)}, f32[2]{0:T(128)}, u32[]{:S(2)}) copy-start(f32[2]{0:T(128)} %param.14) | copy-start | bytes 28
  28.3 13.7 %copy-start.12 = (s32[2,16]{1,0:T(2,128)S(1)}, s32[2,16]{1,0:T(2,128)}, u32[]{:S(2)}) copy-start(s32[2,16]{1,0:T(2,128)} %param.13) | copy-start | bytes 388
  29.3 28.1 %collective-permute-start.5 = (f32[5,16,8,1]{3,1,2,0:T(8,128)}, f32[5,16,8,1]{3,1,2,0:T(8,128)S(1)}, u32[]{:S(2)}, u32[]{:S(2)}) collective-permute-start(f32[5,16,8,1]{3,1,2,0:T(8,128)} %get-tuple-element.45), channel_id=1, source_target_pairs={{0,1},{1,0},{2,3},{3,2},{4,5},{5,4},{6,7},{7,6},{8,9},{9,8},{10,11... | collective-permute-start | bytes 7688 | tf_op jit(solution)/shard_map/ppermute | solution.py:49
  36.7 19.6 %collective-permute-start.4 = (f32[5,16,8,1]{3,1,2,0:T(8,128)}, f32[5,16,8,1]{3,1,2,0:T(8,128)}, u32[]{:S(2)}, u32[]{:S(2)}) collective-permute-start(f32[5,16,8,1]{3,1,2,0:T(8,128)} %get-tuple-element.44), channel_id=1, source_target_pairs={{1,0},{0,1},{3,2},{2,3},{5,4},{4,5},{7,6},{6,7},{9,8},{8,9},{11,10... | collective-permute-start | bytes 7688 | tf_op jit(solution)/shard_map/ppermute | solution.py:52
  59.1 1.1 copy-start
  60.2 1.1 copy-start.2
  99.9 12.2 %copy-start.5 = (f32[24,512]{1,0:T(8,128)}, f32[24,512]{1,0:T(8,128)S(1)}, u32[]{:S(2)}) copy-start(f32[24,512]{1,0:T(8,128)S(1)} %fusion) | copy-start | bytes 147460
  99.9 12.8 %collective-permute-start.6 = (f32[24,512]{1,0:T(8,128)S(1)}, f32[24,512]{1,0:T(8,128)}, u32[]{:S(2)}, u32[]{:S(2)}) collective-permute-start(f32[24,512]{1,0:T(8,128)S(1)} %fusion), channel_id=1, source_target_pairs={{0,2},{2,4},{4,6},{6,8},{8,10},{10,12},{12,14},{1,3},{3,5},{5,7},{... | collective-permute-start | bytes 147464
  103.1 9.0 %collective-permute-start.7 = (f32[4,512]{1,0:T(4,128)S(1)}, f32[4,512]{1,0:T(4,128)S(1)}, u32[]{:S(2)}, u32[]{:S(2)}) collective-permute-start(f32[4,512]{1,0:T(4,128)S(1)} %slice.292), channel_id=1, source_target_pairs={{0,4},{2,6},{4,8},{6,10},{8,12},{10,14},{1,5},{3,7},{5,9},{7,11},{... | collective-permute-start | bytes 24584
  105.7 29.1 %collective-permute-start.2 = (f32[5,18,1,512]{3,1,2,0:T(8,128)}, f32[5,18,1,512]{3,1,2,0:T(8,128)}, u32[]{:S(2)}, u32[]{:S(2)}) collective-permute-start(f32[5,18,1,512]{3,1,2,0:T(8,128)} %get-tuple-element.37), channel_id=1, source_target_pairs={{2,0},{4,2},{6,4},{8,6},{10,8},{12,10},{14,12},{3,1},{5,3},{7,5},{... | collective-permute-start | bytes 552968 | tf_op jit(solution)/shard_map/ppermute | solution.py:52
  110.2 24.6 %collective-permute-start.3 = (f32[5,18,1,512]{3,1,2,0:T(8,128)}, f32[5,18,1,512]{3,1,2,0:T(8,128)}, u32[]{:S(2)}, u32[]{:S(2)}) collective-permute-start(f32[5,18,1,512]{3,1,2,0:T(8,128)} %get-tuple-element.36), channel_id=1, source_target_pairs={{0,2},{2,4},{4,6},{6,8},{8,10},{10,12},{12,14},{1,3},{3,5},{5,7},{... | collective-permute-start | bytes 552968 | tf_op jit(solution)/shard_map/ppermute | solution.py:49
  112.1 0.6 copy-start.6
  115.2 19.6 %copy-start.7 = (pred[8]{0:T(512)(128)(4,1)S(1)}, pred[8]{0:T(512)(128)(4,1)}, u32[]{:S(2)}) copy-start(pred[8]{0:T(512)(128)(4,1)} %get-tuple-element.60) | copy-start | bytes 28
  115.2 19.6 %copy-start.8 = (pred[8]{0:T(512)(128)(4,1)S(1)}, pred[8]{0:T(512)(128)(4,1)}, u32[]{:S(2)}) copy-start(pred[8]{0:T(512)(128)(4,1)} %get-tuple-element.61) | copy-start | bytes 28
  115.2 19.6 %copy-start.9 = (pred[16]{0:T(512)(128)(4,1)S(1)}, pred[16]{0:T(512)(128)(4,1)}, u32[]{:S(2)}) copy-start(pred[16]{0:T(512)(128)(4,1)} %get-tuple-element.62) | copy-start | bytes 52
  115.2 19.6 %copy-start.10 = (pred[16]{0:T(512)(128)(4,1)S(1)}, pred[16]{0:T(512)(128)(4,1)}, u32[]{:S(2)}) copy-start(pred[16]{0:T(512)(128)(4,1)} %get-tuple-element.63) | copy-start | bytes 52
  138.0 1.3 copy-start.4
  138.1 1.7 %copy-start.3 = (f32[5,16,8,512]{3,1,2,0:T(8,128)S(1)}, f32[5,16,8,512]{3,1,2,0:T(8,128)}, u32[]{:S(2)}) copy-start(f32[5,16,8,512]{3,1,2,0:T(8,128)} %copy-done.2) | copy-start | bytes 3932164
  138.2 2.0 %copy-start.1 = (f32[5,16,8,512]{3,1,2,0:T(8,128)S(1)}, f32[5,16,8,512]{3,1,2,0:T(8,128)}, u32[]{:S(2)}) copy-start(f32[5,16,8,512]{3,1,2,0:T(8,128)} %copy-done) | copy-start | bytes 3932164
where the time goes:
time: 149 us; the launch traced here: 147 us
  blocking collectives  42.2 us (28%)
  starting transfers between devices  40.3 us (27%)
  local copies, waits for them, and re-layouts  29.5 us (20%)
  other arithmetic  16.5 us (11%)
  matrix products  10 us (7%)
  waiting for transfers between devices  7.48 us (5%)
    unnamed x1, blocking collectives  25.7 us
    all_gather x1, blocking collectives, sum_by_parts(): whole = lax.all_gather(own, axis, axis=0, tiled=True)  16.5 us
    ppermute x3, starting transfers between devices, extended(): lax.ppermute(lax.slice_in_dim(block, block.shape[dim] - width, None, axis...  14 us
    all_to_all x1, starting transfers between devices, moved(): lax.all_to_all(group, axis, split_axis=split_dim, concat_axis=concat_dim,...  13.8 us
    unnamed x36, local copies, waits for them, and re-layouts  10.5 us
    ppermute x3, starting transfers between devices, extended(): lax.ppermute(lax.slice_in_dim(block, 0, width, axis=dim), axis, backward)  7.66 us
    ppermute x3, waiting for transfers between devices, extended(): lax.ppermute(lax.slice_in_dim(block, 0, width, axis=dim), axis, backward)  7.46 us
    dot_general x1, matrix products, evaluate(): jnp.einsum('ft,nfktvs->nfkvs', basis_pair, slot_block, precision=lax.Prec...  5.95 us
  transfers between devices with their start and end apart: 9, of which 1 were waited for; matrix products, arithmetic and copies ran while one was open for 17% of the time, Pallas kernels for 0%

commit v1 on v0

v1 whole, which is shorter than its diff:
```python
import functools

import jax
import jax.numpy as jnp
from jax import lax
from jax.experimental import pallas as pl
from jax.experimental.pallas import tpu as pltpu
from jax.sharding import PartitionSpec as P

MESH = pl.DeviceIdType.MESH
LANES = 128


def pressure_of(u):
    kinetic = 0.5 * (u[1] * u[1] + u[2] * u[2] + u[3] * u[3]) / u[0]
    return 0.4 * (u[4] - kinetic)


def flux_of(u, pressure, direction):
    velocity = u[direction] / u[0]
    parts = [u[direction], u[1] * velocity, u[2] * velocity, u[3] * velocity, (u[4] + pressure) * velocity]
    parts[direction] = parts[direction] + pressure
    return parts


def as_previous(u, flux):
    return [0.125 * a + 0.25 * f for a, f in zip(u, flux)]


def as_next(u, flux):
    return [0.125 * a - 0.25 * f for a, f in zip(u, flux)]


def kernel(
    sizes, flow, step, lower_coef, upper_coef, basis, partner, periodic, acc_out, delta_out,
    fx, sx, coef, part, rx_core, rx_chain, total, slots, recv, edge, halo, halo_in, span_tx, span_rx, span_in,
    out_v, ghost, delta, table,
    load_sem, core_send, core_recv, chain_send, chain_recv, row_send, row_recv,
    axial_send, axial_recv, pitch_send, pitch_recv, span_send, span_recv, store_sem, delta_sem,
):
    n_axial, n_pitch, n_span, n_var, n_row, n_col, n_cell, n_term = sizes
    at = lax.axis_index("axial")
    pitch = lax.axis_index("pitch")
    span = lax.axis_index("span")
    chips = n_pitch // 2
    core = lax.rem(pitch, 2)
    chip = lax.div(pitch, 2)
    place = jnp.where(core == 0, chips - 1 - chip, chip)
    step_to = jnp.where(core == 0, pitch - 2, pitch + 2)
    is_end = place == chips - 1
    mate = pitch + 1 - 2 * core
    beside = pitch - 1 + 2 * core
    has_beside = (beside >= 0) & (beside < n_pitch)
    tail = n_cell - LANES
    first_blade, end_blade = n_axial // 4, 3 * n_axial // 4

    def is_blade(a):
        return (a >= first_blade) & (a < end_blade)

    def load_coef(face):
        return [
            pltpu.make_async_copy(upper_coef, coef.at[0], load_sem.at[0]),
            pltpu.make_async_copy(lower_coef, coef.at[1], load_sem.at[1]),
        ][face]

    load_flow = pltpu.make_async_copy(flow, fx.at[:, pl.ds(1, n_row)], load_sem.at[2])
    load_step = pltpu.make_async_copy(step, sx, load_sem.at[3])
    load_coef(0).start()
    load_coef(1).start()
    load_flow.start()
    load_step.start()

    barrier = pltpu.get_barrier_semaphore()

    def greet(**where):
        pl.semaphore_signal(barrier, inc=1, device_id=where, device_id_type=MESH)

    greet(pitch=mate)

    @pl.when(has_beside)
    def _():
        greet(pitch=beside)

    @pl.when(pitch >= 2)
    def _():
        greet(pitch=pitch - 2)

    @pl.when(pitch < n_pitch - 2)
    def _():
        greet(pitch=pitch + 2)

    greet(span=1 - span)

    @pl.when(is_end)
    def _():
        @pl.loop(1, n_axial)
        def _(j):
            greet(axial=lax.rem(at + j, n_axial))

    @pl.when(jnp.logical_not(is_end) & (at > 0))
    def _():
        greet(axial=at - 1)

    @pl.when(jnp.logical_not(is_end) & (at < n_axial - 1))
    def _():
        greet(axial=at + 1)

    one = jnp.int32(1)
    zero = jnp.int32(0)
    near = jnp.where(at > 0, one, zero) + jnp.where(at < n_axial - 1, one, zero)
    greetings = (
        2
        + jnp.where(has_beside, one, zero)
        + jnp.where(pitch >= 2, one, zero)
        + jnp.where(pitch < n_pitch - 2, one, zero)
        + jnp.where(is_end, n_axial - 1, near)
    )

    def evaluate(face, v):
        value = basis[face, 0] * coef[face, 0, v]
        for t in range(1, n_term):
            value = value + basis[face, t] * coef[face, t, v]
        part[face, v] = value

    load_coef(0).wait()
    load_coef(1).wait()
    for v in range(n_var):
        evaluate(1 - core, v)

    pl.semaphore_wait(barrier, greetings)

    def core_copy(v):
        return pltpu.make_async_remote_copy(
            src_ref=part.at[1 - core, v], dst_ref=rx_core.at[v], send_sem=core_send.at[v], recv_sem=core_recv.at[v],
            device_id={"pitch": mate}, device_id_type=MESH)

    for v in range(n_var):
        core_copy(v).start()

    load_flow.wait()

    def axial_up():
        return pltpu.make_async_remote_copy(
            src_ref=fx.at[:, n_row], dst_ref=fx.at[:, 0], send_sem=axial_send.at[0], recv_sem=axial_recv.at[0],
            device_id={"axial": at + 1}, device_id_type=MESH)

    def axial_down():
        return pltpu.make_async_remote_copy(
            src_ref=fx.at[:, 1], dst_ref=fx.at[:, n_row + 1], send_sem=axial_send.at[1], recv_sem=axial_recv.at[1],
            device_id={"axial": at - 1}, device_id_type=MESH)

    @pl.when(at < n_axial - 1)
    def _():
        axial_up().start()

    @pl.when(at > 0)
    def _():
        axial_down().start()

    for v in range(n_var):
        evaluate(core, v)

    def chain_copy(v):
        return pltpu.make_async_remote_copy(
            src_ref=total.at[v], dst_ref=rx_chain.at[v], send_sem=chain_send.at[v], recv_sem=chain_recv.at[v],
            device_id={"pitch": step_to}, device_id_type=MESH)

    for v in range(n_var):
        core_copy(v).wait_recv()
        total[v] = part[core, v] + rx_core[v]

        @pl.when(place > 0)
        def _():
            chain_copy(v).wait_recv()
            total[v] = total[v] + rx_chain[v]

        @pl.when(jnp.logical_not(is_end))
        def _():
            chain_copy(v).start()

    def row_copy(target):
        return pltpu.make_async_remote_copy(
            src_ref=slots.at[target], dst_ref=recv.at[at], send_sem=row_send, recv_sem=row_recv,
            device_id={"axial": target}, device_id_type=MESH)

    def tip_copy(target):
        return pltpu.make_async_remote_copy(
            src_ref=slots.at[target, :, :, pl.ds(tail, LANES)], dst_ref=recv.at[at, :, :, pl.ds(tail, LANES)],
            send_sem=row_send, recv_sem=row_recv, device_id={"axial": target}, device_id_type=MESH)

    @pl.when(is_end)
    def _():
        @pl.loop(0, n_axial)
        def _(d):
            index = jnp.int32(0)
            for r in range(n_row):
                index = jnp.where(lax.div(partner[1 - core, r], n_row) == d, r, index)
            table[d] = index

        @pl.loop(1, n_axial)
        def _(j):
            target = lax.rem(at + j, n_axial)
            row = table[target]
            for v in range(n_var):
                slots[target, v] = total[v, pl.ds(row, 1), :]

            @pl.when(jnp.logical_not(is_blade(target)))
            def _():
                row_copy(target).start()

            @pl.when(is_blade(target) & (span == n_span - 1))
            def _():
                tip_copy(target).start()

        own = table[at]
        for v in range(n_var):
            recv[at, v] = total[v, pl.ds(own, 1), :]

    lane = lax.broadcasted_iota(jnp.int32, (n_col, LANES), 1)

    def pack(i, carry):
        low, high = carry
        for v in range(n_var):
            spot = v * n_row + i
            last = pltpu.roll(fx[v, i + 1, :, pl.ds(tail, LANES)], spot + 1, 1)
            first = pltpu.roll(fx[v, i + 1, :, pl.ds(0, LANES)], spot, 1)
            low = jnp.where(lane == spot, last, low)
            high = jnp.where(lane == spot, first, high)
            edge[0, v, pl.ds(i, 1), :] = fx[v, i + 1, pl.ds(0, 1), :]
            edge[1, v, pl.ds(i, 1), :] = fx[v, i + 1, pl.ds(n_col - 1, 1), :]
        return low, high

    blank = jnp.ones((n_col, LANES), jnp.float32)
    low, high = lax.fori_loop(0, n_row, pack, (blank, blank))
    span_tx[0] = low
    span_tx[1] = high

    span_copy = pltpu.make_async_remote_copy(
        src_ref=span_tx, dst_ref=span_rx, send_sem=span_send, recv_sem=span_recv,
        device_id={"span": 1 - span}, device_id_type=MESH)
    span_copy.start()

    def pitch_up():
        return pltpu.make_async_remote_copy(
            src_ref=edge.at[1], dst_ref=halo.at[0], send_sem=pitch_send.at[0], recv_sem=pitch_recv.at[0],
            device_id={"pitch": pitch + 1}, device_id_type=MESH)

    def pitch_down():
        return pltpu.make_async_remote_copy(
            src_ref=edge.at[0], dst_ref=halo.at[1], send_sem=pitch_send.at[1], recv_sem=pitch_recv.at[1],
            device_id={"pitch": pitch - 1}, device_id_type=MESH)

    @pl.when(pitch < n_pitch - 1)
    def _():
        pitch_up().start()

    @pl.when(pitch > 0)
    def _():
        pitch_down().start()

    @pl.when(at > 0)
    def _():
        axial_up().wait_recv()

    @pl.when(at == 0)
    def _():
        for v in range(n_var):
            fx[v, 0] = fx[v, 1]

    @pl.when(at < n_axial - 1)
    def _():
        axial_down().wait_recv()

    @pl.when(at == n_axial - 1)
    def _():
        for v in range(n_var):
            fx[v, n_row + 1] = fx[v, n_row]

    @pl.when(pitch > 0)
    def _():
        pitch_up().wait_recv()
        u = [halo[0, v] for v in range(n_var)]
        for v, value in enumerate(as_previous(u, flux_of(u, pressure_of(u), 2))):
            halo_in[0, v] = value

    @pl.when(pitch == 0)
    def _():
        for v in range(n_var):
            halo_in[0, v] = jnp.zeros((n_row, n_cell), jnp.float32)

    @pl.when(pitch < n_pitch - 1)
    def _():
        pitch_down().wait_recv()
        u = [halo[1, v] for v in range(n_var)]
        for v, value in enumerate(as_next(u, flux_of(u, pressure_of(u), 2))):
            halo_in[1, v] = value

    @pl.when(pitch == n_pitch - 1)
    def _():
        for v in range(n_var):
            halo_in[1, v] = jnp.zeros((n_row, n_cell), jnp.float32)

    span_copy.wait_recv()
    for side, form in enumerate((as_previous, as_next)):
        u = [span_rx[side]]
        for v in range(1, n_var):
            u.append(pltpu.roll(span_rx[side], LANES - v * n_row, 1))
        for v, value in enumerate(form(u, flux_of(u, pressure_of(u), 3))):
            span_in[side, v] = value

    load_step.wait()
    cell = lax.broadcasted_iota(jnp.int32, (n_col, n_cell), 1)
    col = lax.broadcasted_iota(jnp.int32, (n_col, n_cell), 0)

    def stencil(i, carry):
        before = [fx[v, i] for v in range(n_var)]
        after = [fx[v, i + 2] for v in range(n_var)]
        flux_before = flux_of(before, pressure_of(before), 1)
        flux_after = flux_of(after, pressure_of(after), 1)
        for v in range(n_var):
            out_v[v, i] = sx[v, i] + 0.125 * (before[v] + after[v]) + 0.25 * (flux_before[v] - flux_after[v])
        u = [fx[v, i + 1] for v in range(n_var)]
        p = pressure_of(u)
        flux = flux_of(u, p, 2)
        above = as_next(u, flux)
        below = as_previous(u, flux)
        for v in range(n_var):
            down = jnp.where(col == 0, halo_in[0, v, pl.ds(i, 1), :], pltpu.roll(below[v], 1, 0))
            up = jnp.where(col == n_col - 1, halo_in[1, v, pl.ds(i, 1), :], pltpu.roll(above[v], n_col - 1, 0))
            out_v[v, i] = out_v[v, i] + down + up - 0.75 * u[v]
        flux = flux_of(u, p, 3)
        above = as_next(u, flux)
        below = as_previous(u, flux)
        for v in range(n_var):
            first = pltpu.roll(span_in[0, v], LANES - i, 1)[:, :1]
            last = pltpu.roll(span_in[1, v], LANES - i, 1)[:, :1]
            down = jnp.where(cell == 0, first, pltpu.roll(below[v], 1, 1))
            up = jnp.where(cell == n_cell - 1, last, pltpu.roll(above[v], n_cell - 1, 1))
            out_v[v, i] = out_v[v, i] + down + up
        return carry

    lax.fori_loop(0, n_row, stencil, 0)
    store = pltpu.make_async_copy(out_v, acc_out, store_sem)
    store.start()

    @pl.when(is_end)
    def _():
        blade = is_blade(at)

        @pl.when(jnp.logical_not(blade))
        def _():
            pltpu.make_async_copy(
                slots.at[pl.ds(0, n_axial - 1)], recv.at[pl.ds(0, n_axial - 1)], row_recv).wait()

        @pl.when(blade & (span == n_span - 1))
        def _():
            pltpu.make_async_copy(
                slots.at[pl.ds(0, n_axial - 1), :, :, pl.ds(tail, LANES)],
                recv.at[pl.ds(0, n_axial - 1), :, :, pl.ds(tail, LANES)], row_recv).wait()

        position = lax.broadcasted_iota(jnp.int32, (1, n_cell), 1) + span * n_cell

        @pl.loop(0, n_row)
        def _(i):
            source = lax.div(partner[core, i], n_row)
            is_open = position >= n_span * n_cell - periodic[core, i]
            for v in range(n_var):
                wall = edge[core, v, pl.ds(i, 1), :]
                if v == 2:
                    wall = -wall
                ghost[v, pl.ds(i, 1), :] = jnp.where(is_open, recv[source, v], wall)

        u = [ghost[v] for v in range(n_var)]
        flux = flux_of(u, pressure_of(u), 2)
        sign = jnp.where(core == 0, 0.25, -0.25)
        for v in range(n_var):
            delta[v] = 0.125 * u[v] + sign * flux[v]

    @pl.when(jnp.logical_not(is_end))
    def _():
        for v in range(n_var):
            delta[v] = jnp.zeros((n_row, n_cell), jnp.float32)

    store_delta = pltpu.make_async_copy(delta, delta_out, delta_sem)
    store_delta.start()

    for v in range(n_var):
        core_copy(v).wait_send()

    @pl.when(jnp.logical_not(is_end))
    def _():
        for v in range(n_var):
            chain_copy(v).wait_send()

    @pl.when(is_end)
    def _():
        @pl.loop(1, n_axial)
        def _(j):
            target = lax.rem(at + j, n_axial)

            @pl.when(jnp.logical_not(is_blade(target)))
            def _():
                row_copy(target).wait_send()

            @pl.when(is_blade(target) & (span == n_span - 1))
            def _():
                tip_copy(target).wait_send()

    @pl.when(at < n_axial - 1)
    def _():
        axial_up().wait_send()

    @pl.when(at > 0)
    def _():
        axial_down().wait_send()

    @pl.when(pitch < n_pitch - 1)
    def _():
        pitch_up().wait_send()

    @pl.when(pitch > 0)
    def _():
        pitch_down().wait_send()

    span_copy.wait_send()
    store.wait()
    store_delta.wait()


def term_basis(phase_value, term_ids):
    harmonic = ((term_ids + 1) // 2).astype(phase_value.dtype)
    return jnp.where(
        (term_ids % 2 == 0) & (term_ids > 0), jnp.sin(harmonic * phase_value), jnp.cos(harmonic * phase_value))


def per_device(flow, step, lower_coef, upper_coef, partner, periodic, phase_angles):
    n_axial = lax.axis_size("axial")
    n_pitch = lax.axis_size("pitch")
    n_span = lax.axis_size("span")
    n_var, n_row, n_col, n_cell = flow.shape
    n_term = lower_coef.shape[0]
    pitch = lax.axis_index("pitch")
    term_ids = pitch * n_term + jnp.arange(n_term, dtype=jnp.int32)
    basis = term_basis(phase_angles[:, None], term_ids[None, :])
    sizes = (n_axial, n_pitch, n_span, n_var, n_row, n_col, n_cell, n_term)
    any_spec = pl.BlockSpec(memory_space=pl.ANY)
    smem = pl.BlockSpec(memory_space=pltpu.SMEM)
    face = (n_var, n_row, n_cell)
    f32 = jnp.float32
    dma = pltpu.SemaphoreType.DMA
    acc, delta = pl.pallas_call(
        functools.partial(kernel, sizes),
        out_shape=(jax.ShapeDtypeStruct(flow.shape, f32), jax.ShapeDtypeStruct(face, f32)),
        in_specs=[any_spec] * 4 + [smem] * 3,
        out_specs=(any_spec, any_spec),
        scratch_shapes=[
            pltpu.VMEM((n_var, n_row + 2, n_col, n_cell), f32),
            pltpu.VMEM(flow.shape, f32),
            pltpu.VMEM((2, n_term, *face), f32),
            pltpu.VMEM((2, *face), f32),
            pltpu.VMEM(face, f32),
            pltpu.VMEM(face, f32),
            pltpu.VMEM(face, f32),
            pltpu.VMEM((n_axial, n_var, 1, n_cell), f32),
            pltpu.VMEM((n_axial, n_var, 1, n_cell), f32),
            pltpu.VMEM((2, *face), f32),
            pltpu.VMEM((2, *face), f32),
            pltpu.VMEM((2, *face), f32),
            pltpu.VMEM((2, n_col, LANES), f32),
            pltpu.VMEM((2, n_col, LANES), f32),
            pltpu.VMEM((2, n_var, n_col, LANES), f32),
            pltpu.VMEM(flow.shape, f32),
            pltpu.VMEM(face, f32),
            pltpu.VMEM(face, f32),
            pltpu.SMEM((n_axial,), jnp.int32),
            dma((4,)), dma((n_var,)), dma((n_var,)), dma((n_var,)), dma((n_var,)), dma, dma,
            dma((2,)), dma((2,)), dma((2,)), dma((2,)), dma, dma, dma, dma,
        ],
        compiler_params=pltpu.CompilerParams(collective_id=0, has_side_effects=True),
        name="section",
    )(flow, step, lower_coef, upper_coef, basis, partner, periodic)
    edge_col = jnp.where(pitch == 0, 0, n_col - 1)
    col = lax.broadcasted_iota(jnp.int32, (1, 1, n_col, 1), 2)
    return acc + jnp.where(col == edge_col, delta[:, :, None, :], 0.0)


def solution(mesh):
    in_specs = (
        P(None, "axial", "pitch", "span"),
        P(None, "axial", "pitch", "span"),
        P("pitch", None, "axial", "span"),
        P("pitch", None, "axial", "span"),
        P(None, "axial"),
        P(None, "axial"),
        P(),
    )
    out_specs = P(None, "axial", "pitch", "span")
    return jax.shard_map(
        per_device, mesh=mesh, in_specs=in_specs, out_specs=out_specs, check_vma=False
    )
```

time: 149 us -> 41 us (0.28)
  the two profiles are of different devices: /device:TPU:1 before, /device:TPU:64 now
where the time goes in v1:
time: 41 us; the launch traced here: 40.9 us
  Pallas kernels  36.8 us (90%)
  other arithmetic  4.05 us (10%)
    pallas_call x1, Pallas kernels, per_device(): pl.pallas_call(functools.partial(kernel, sizes), out_shape=(jax.ShapeDtyp...  36.8 us
    add x1, other arithmetic, per_device(): return acc + jnp.where(col == edge_col, delta[:, :, None, :], 0.0)  2.69 us
    select_n x1, other arithmetic, term_basis(): jnp.where((term_ids % 2 == 0) & (term_ids > 0), jnp.sin(harmonic * phase_...  1.33 us

profile of v1, /device:TPU:64, one launch (start us, length us, event | category | flops | bytes accessed | tf_op | source)
XLA Modules:
  0.0 40.9 jit_solution(1292280052827977937)
XLA Ops:
  0.0 1.3 %fusion.basis = f32[2,2]{1,0:T(2,128)} fusion(pred[2]{0:T(512)(128)(4,1)S(1)} %compare_and_fusion, f32[2]{0:T(128)S(1)} %fusion.2, f32[2]{0:T(128)} %param.13), kind=kLoop, calls=%fused_computation.11 | loop fusion | flops 8 | bytes 34 | tf_op jit(solution)/shard_map/jit(_where)/select_n | solution.py:432
  1.4 36.8 %section.1 = (f32[5,16,8,512]{3,2,1,0:T(8,128)}, f32[5,16,512]{2,1,0:T(8,128)}) custom-call(f32[5,16,8,512]{3,2,1,0:T(8,128)} %flow.1, f32[5,16,8,512]{3,2,1,0:T(8,128)} %step.1, f32[2,5,16,512]{3,2,1,0:T(8,128)} %lower_coef.1, f32[2,5,16,512]{3,2,1,0:T(8,128)} %upper_coef.1, f32[2,2]{1,0:T(2,128)} %fusion.basis, s32[2,16]{1,0:T(2,128)} %partner.1, ...), custom_call_target="tpu_custom_call" | custom-call | tf_op jit(solution)/shard_map/section/pallas_call | solution.py:451
  38.2 2.7 %select_add_fusion = f32[5,16,8,512]{3,2,1,0:T(8,128)} fusion(f32[5,16,8,512]{3,2,1,0:T(8,128)} %get-tuple-element.7, f32[5,16,512]{2,1,0:T(8,128)} %get-tuple-element.8, pred[8]{0:T(512)(128)(4,1)S(1)} %iota_compare_fusion), kind=kLoop, calls=%fused_computation | loop fusion | flops 655360 | bytes 2785288 | tf_op jit(solution)/shard_map/add | solution.py:484
  (3 shorter events, 0.0 us)

commit v2 on v1

v2 whole, which is shorter than its diff:
```python
import functools

import jax
import jax.numpy as jnp
from jax import lax
from jax.experimental import pallas as pl
from jax.experimental.pallas import tpu as pltpu
from jax.sharding import PartitionSpec as P

MESH = pl.DeviceIdType.MESH
LANES = 128


def pressure_of(u):
    kinetic = 0.5 * (u[1] * u[1] + u[2] * u[2] + u[3] * u[3]) / u[0]
    return 0.4 * (u[4] - kinetic)


def flux_of(u, pressure, direction):
    velocity = u[direction] / u[0]
    parts = [u[direction], u[1] * velocity, u[2] * velocity, u[3] * velocity, (u[4] + pressure) * velocity]
    parts[direction] = parts[direction] + pressure
    return parts


def as_previous(u, flux):
    return [0.125 * a + 0.25 * f for a, f in zip(u, flux)]


def as_next(u, flux):
    return [0.125 * a - 0.25 * f for a, f in zip(u, flux)]


def kernel(
    sizes, flow, step, lower_coef, upper_coef, phases, partner, periodic, out_v, sides,
    fx, sx, coef, part, rx_core, rx_near, rx_far, total, slots, recv, edge, halo, span_tx, span_rx, span_in,
    ghost, table,
    load_sem, core_send, core_recv, near_send, near_recv, far_send, far_recv, row_send, row_recv,
    axial_send, axial_recv, pitch_send, pitch_recv, span_send, span_recv, ready,
):
    n_axial, n_pitch, n_span, n_var, n_row, n_col, n_cell, n_term = sizes
    at = lax.axis_index("axial")
    pitch = lax.axis_index("pitch")
    span = lax.axis_index("span")
    chips = n_pitch // 2
    core = lax.rem(pitch, 2)
    chip = lax.div(pitch, 2)
    place = jnp.where(core == 0, chips - 1 - chip, chip)
    toward = 1 - 2 * core
    is_end = place == chips - 1
    is_helper = place == chips - 2
    is_middle = place == chips - 3
    is_start = place == chips - 4
    end = jnp.where(core == 0, 0, n_pitch - 1)
    helper = end + 2 * toward
    middle = end + 4 * toward
    mate = pitch + 1 - 2 * core
    beside = pitch - 1 + 2 * core
    has_beside = (beside >= 0) & (beside < n_pitch)
    tail = n_cell - LANES
    first_blade, end_blade = n_axial // 4, 3 * n_axial // 4

    def is_blade(a):
        return (a >= first_blade) & (a < end_blade)

    def load_coef(face):
        return [
            pltpu.make_async_copy(upper_coef, coef.at[0], load_sem.at[0]),
            pltpu.make_async_copy(lower_coef, coef.at[1], load_sem.at[1]),
        ][face]

    load_flow = pltpu.make_async_copy(flow, fx.at[:, pl.ds(1, n_row)], load_sem.at[2])
    load_step = pltpu.make_async_copy(step, sx, load_sem.at[3])
    @pl.when(core == 0)
    def _():
        load_coef(1).start()
        load_coef(0).start()

    @pl.when(core == 1)
    def _():
        load_coef(0).start()
        load_coef(1).start()

    load_flow.start()
    load_step.start()

    barrier = pltpu.get_barrier_semaphore()

    def greet(**where):
        pl.semaphore_signal(barrier, inc=1, device_id=where, device_id_type=MESH)

    one = jnp.int32(1)
    zero = jnp.int32(0)

    @pl.when(is_end)
    def _():
        @pl.loop(1, n_axial)
        def _(j):
            greet(axial=lax.rem(at + j, n_axial), pitch=helper)

    greetings = jnp.where(is_helper, n_axial - 1, 0)
    for holds, where in (
        (None, {"pitch": mate}),
        (None, {"span": 1 - span}),
        (has_beside, {"pitch": beside}),
        (pitch >= 2, {"pitch": pitch - 2}),
        (pitch < n_pitch - 2, {"pitch": pitch + 2}),
        (is_middle, {"pitch": end}),
        (is_end, {"pitch": middle}),
        (at > 0, {"axial": at - 1}),
        (at < n_axial - 1, {"axial": at + 1}),
    ):
        if holds is None:
            greet(**where)
            greetings = greetings + 1
        else:
            pl.when(holds)(functools.partial(greet, **where))
            greetings = greetings + jnp.where(holds, one, zero)

    spot = lax.broadcasted_iota(jnp.int32, (8, LANES), 1)
    second = spot >= n_term
    term = pitch * n_term + jnp.where(second, spot - n_term, spot)
    angle = lax.shift_right_logical(term + 1, 1).astype(jnp.float32) * jnp.where(second, phases[1], phases[0])
    basis = jnp.where((lax.rem(term, 2) == 0) & (term > 0), jnp.sin(angle), jnp.cos(angle))

    def evaluate(face, v):
        first = jnp.where(face == 0, basis, pltpu.roll(basis, LANES - n_term, 1))
        value = first[:1, :1] * coef[face, 0, v]
        for t in range(1, n_term):
            value = value + first[:1, t : t + 1] * coef[face, t, v]
        part[face, v] = value

    load_coef(0).wait()
    load_coef(1).wait()
    for v in range(n_var):
        evaluate(1 - core, v)

    pl.semaphore_wait(barrier, greetings)

    def core_copy(v):
        return pltpu.make_async_remote_copy(
            src_ref=part.at[1 - core, v], dst_ref=rx_core.at[v], send_sem=core_send.at[v], recv_sem=core_recv.at[v],
            device_id={"pitch": mate}, device_id_type=MESH)

    for v in range(n_var):
        core_copy(v).start()

    @pl.when(is_helper)
    def _():
        pl.semaphore_signal(ready, inc=1, device_id={"pitch": end}, device_id_type=MESH)

    for v in range(n_var):
        evaluate(core, v)

    load_flow.wait()

    def axial_up():
        return pltpu.make_async_remote_copy(
            src_ref=fx.at[:, n_row], dst_ref=fx.at[:, 0], send_sem=axial_send.at[0], recv_sem=axial_recv.at[0],
            device_id={"axial": at + 1}, device_id_type=MESH)

    def axial_down():
        return pltpu.make_async_remote_copy(
            src_ref=fx.at[:, 1], dst_ref=fx.at[:, n_row + 1], send_sem=axial_send.at[1], recv_sem=axial_recv.at[1],
            device_id={"axial": at - 1}, device_id_type=MESH)

    @pl.when(at < n_axial - 1)
    def _():
        axial_up().start()

    @pl.when(at > 0)
    def _():
        axial_down().start()

    lane = lax.broadcasted_iota(jnp.int32, (n_col, LANES), 1)
    span_copy = pltpu.make_async_remote_copy(
        src_ref=span_tx, dst_ref=span_rx, send_sem=span_send, recv_sem=span_recv,
        device_id={"span": 1 - span}, device_id_type=MESH)

    def pitch_up():
        return pltpu.make_async_remote_copy(
            src_ref=edge.at[1], dst_ref=halo.at[0], send_sem=pitch_send.at[0], recv_sem=pitch_recv.at[0],
            device_id={"pitch": pitch + 1}, device_id_type=MESH)

    def pitch_down():
        return pltpu.make_async_remote_copy(
            src_ref=edge.at[0], dst_ref=halo.at[1], send_sem=pitch_send.at[1], recv_sem=pitch_recv.at[1],
            device_id={"pitch": pitch - 1}, device_id_type=MESH)

    def pack(i, carry):
        low, high = carry
        for v in range(n_var):
            spot = v * n_row + i
            last = pltpu.roll(fx[v, i + 1, :, pl.ds(tail, LANES)], spot + 1, 1)
            first = pltpu.roll(fx[v, i + 1, :, pl.ds(0, LANES)], spot, 1)
            low = jnp.where(lane == spot, last, low)
            high = jnp.where(lane == spot, first, high)
            edge[0, v, pl.ds(i, 1), :] = fx[v, i + 1, pl.ds(0, 1), :]
            edge[1, v, pl.ds(i, 1), :] = fx[v, i + 1, pl.ds(n_col - 1, 1), :]
        return low, high

    def send_edges():
        blank = jnp.ones((n_col, LANES), jnp.float32)
        low, high = lax.fori_loop(0, n_row, pack, (blank, blank))
        span_tx[0] = low
        span_tx[1] = high
        span_copy.start()
        pl.when(core == 0)(lambda: pitch_up().start())
        pl.when(core == 1)(lambda: pitch_down().start())
        pl.when((core == 0) & (pitch > 0))(lambda: pitch_down().start())
        pl.when((core == 1) & (pitch < n_pitch - 1))(lambda: pitch_up().start())

    early = is_end | is_middle
    pl.when(early)(send_edges)

    @pl.when(is_end)
    def _():
        @pl.loop(0, n_axial)
        def _(d):
            index = jnp.int32(0)
            for r in range(n_row):
                index = jnp.where(lax.div(partner[1 - core, r], n_row) == d, r, index)
            table[d] = index

    def near_copy(v):
        return pltpu.make_async_remote_copy(
            src_ref=total.at[v], dst_ref=rx_near.at[v], send_sem=near_send.at[v], recv_sem=near_recv.at[v],
            device_id={"pitch": pitch - 2 * toward}, device_id_type=MESH)

    def far_copy(v):
        return pltpu.make_async_remote_copy(
            src_ref=total.at[v], dst_ref=rx_far.at[v], send_sem=far_send.at[v], recv_sem=far_recv.at[v],
            device_id={"pitch": end}, device_id_type=MESH)

    for v in range(n_var):
        core_copy(v).wait_recv()
        total[v] = part[core, v] + rx_core[v]
        pl.when(is_start | is_helper)(lambda: near_copy(v).start())

    pl.when(jnp.logical_not(early))(send_edges)

    if chips > 2:
        @pl.when(is_middle)
        def _():
            for v in range(n_var):
                if chips > 3:
                    near_copy(v).wait_recv()
                    total[v] = total[v] + rx_near[v]
                far_copy(v).start()

    def row_copy(target):
        return pltpu.make_async_remote_copy(
            src_ref=slots.at[target], dst_ref=recv.at[at], send_sem=row_send, recv_sem=row_recv,
            device_id={"axial": target}, device_id_type=MESH)

    def tip_copy(target):
        return pltpu.make_async_remote_copy(
            src_ref=slots.at[target, :, :, pl.ds(tail, LANES)], dst_ref=recv.at[at, :, :, pl.ds(tail, LANES)],
            send_sem=row_send, recv_sem=row_recv, device_id={"axial": target}, device_id_type=MESH)

    @pl.when(is_end)
    def _():
        for v in range(n_var):
            near_copy(v).wait_recv()
            total[v] = total[v] + rx_near[v]
            if chips > 2:
                far_copy(v).wait_recv()
                total[v] = total[v] + rx_far[v]

            @pl.loop(0, n_axial)
            def _(d):
                slots[d, v] = total[v, pl.ds(table[d], 1), :]

        pl.semaphore_wait(ready, 1)

        @pl.loop(1, n_axial)
        def _(j):
            target = lax.rem(at + j, n_axial)
            pl.when(jnp.logical_not(is_blade(target)))(lambda: row_copy(target).start())
            pl.when(is_blade(target) & (span == n_span - 1))(lambda: tip_copy(target).start())

        own = table[at]
        for v in range(n_var):
            recv[at, v] = total[v, pl.ds(own, 1), :]

    span_copy.wait_recv()

    @pl.when(at > 0)
    def _():
        axial_up().wait_recv()

    @pl.when(at == 0)
    def _():
        for v in range(n_var):
            fx[v, 0] = fx[v, 1]

    @pl.when(at < n_axial - 1)
    def _():
        axial_down().wait_recv()

    @pl.when(at == n_axial - 1)
    def _():
        for v in range(n_var):
            fx[v, n_row + 1] = fx[v, n_row]

    for side, form in enumerate((as_previous, as_next)):
        u = [span_rx[side]]
        for v in range(1, n_var):
            u.append(pltpu.roll(span_rx[side], LANES - v * n_row, 1))
        for v, value in enumerate(form(u, flux_of(u, pressure_of(u), 3))):
            span_in[side, v] = value

    load_step.wait()
    cell = lax.broadcasted_iota(jnp.int32, (n_col, n_cell), 1)
    col = lax.broadcasted_iota(jnp.int32, (n_col, n_cell), 0)

    def stencil(i, carry):
        before = [fx[v, i] for v in range(n_var)]
        after = [fx[v, i + 2] for v in range(n_var)]
        flux_before = flux_of(before, pressure_of(before), 1)
        flux_after = flux_of(after, pressure_of(after), 1)
        for v in range(n_var):
            out_v[v, i] = sx[v, i] + 0.125 * (before[v] + after[v]) + 0.25 * (flux_before[v] - flux_after[v])
        u = [fx[v, i + 1] for v in range(n_var)]
        p = pressure_of(u)
        flux = flux_of(u, p, 2)
        above = as_next(u, flux)
        below = as_previous(u, flux)
        for v in range(n_var):
            down = jnp.where(col == 0, 0.0, pltpu.roll(below[v], 1, 0))
            up = jnp.where(col == n_col - 1, 0.0, pltpu.roll(above[v], n_col - 1, 0))
            out_v[v, i] = out_v[v, i] + down + up - 0.75 * u[v]
        flux = flux_of(u, p, 3)
        above = as_next(u, flux)
        below = as_previous(u, flux)
        for v in range(n_var):
            first = pltpu.roll(span_in[0, v], LANES - i, 1)[:, :1]
            last = pltpu.roll(span_in[1, v], LANES - i, 1)[:, :1]
            down = jnp.where(cell == 0, first, pltpu.roll(below[v], 1, 1))
            up = jnp.where(cell == n_cell - 1, last, pltpu.roll(above[v], n_cell - 1, 1))
            out_v[v, i] = out_v[v, i] + down + up
        return carry

    lax.fori_loop(0, n_row, stencil, 0)

    def add_side(side, u):
        form = (as_previous, as_next)[side]
        for v, value in enumerate(form(u, flux_of(u, pressure_of(u), 2))):
            sides[side, v] = value

    @pl.when(pitch > 0)
    def _():
        pitch_up().wait_recv()
        add_side(0, [halo[0, v] for v in range(n_var)])

    @pl.when(pitch < n_pitch - 1)
    def _():
        pitch_down().wait_recv()
        add_side(1, [halo[1, v] for v in range(n_var)])

    @pl.when(is_end)
    def _():
        blade = is_blade(at)

        @pl.when(jnp.logical_not(blade))
        def _():
            pltpu.make_async_copy(
                slots.at[pl.ds(0, n_axial - 1)], recv.at[pl.ds(0, n_axial - 1)], row_recv).wait()

        @pl.when(blade & (span == n_span - 1))
        def _():
            pltpu.make_async_copy(
                slots.at[pl.ds(0, n_axial - 1), :, :, pl.ds(tail, LANES)],
                recv.at[pl.ds(0, n_axial - 1), :, :, pl.ds(tail, LANES)], row_recv).wait()

        position = lax.broadcasted_iota(jnp.int32, (1, n_cell), 1) + span * n_cell

        @pl.loop(0, n_row)
        def _(i):
            source = lax.div(partner[core, i], n_row)
            is_open = position >= n_span * n_cell - periodic[core, i]
            for v in range(n_var):
                wall = edge[core, v, pl.ds(i, 1), :]
                if v == 2:
                    wall = -wall
                ghost[v, pl.ds(i, 1), :] = jnp.where(is_open, recv[source, v], wall)

        pl.when(core == 0)(lambda: add_side(0, [ghost[v] for v in range(n_var)]))
        pl.when(core == 1)(lambda: add_side(1, [ghost[v] for v in range(n_var)]))

    for v in range(n_var):
        core_copy(v).wait_send()

    @pl.when(is_start | is_helper)
    def _():
        for v in range(n_var):
            near_copy(v).wait_send()

    if chips > 2:
        @pl.when(is_middle)
        def _():
            for v in range(n_var):
                far_copy(v).wait_send()

    @pl.when(is_end)
    def _():
        @pl.loop(1, n_axial)
        def _(j):
            target = lax.rem(at + j, n_axial)

            @pl.when(jnp.logical_not(is_blade(target)))
            def _():
                row_copy(target).wait_send()

            @pl.when(is_blade(target) & (span == n_span - 1))
            def _():
                tip_copy(target).wait_send()

    @pl.when(at < n_axial - 1)
    def _():
        axial_up().wait_send()

    @pl.when(at > 0)
    def _():
        axial_down().wait_send()

    @pl.when(pitch < n_pitch - 1)
    def _():
        pitch_up().wait_send()

    @pl.when(pitch > 0)
    def _():
        pitch_down().wait_send()

    span_copy.wait_send()


def per_device(flow, step, lower_coef, upper_coef, partner, periodic, phase_angles):
    n_axial = lax.axis_size("axial")
    n_pitch = lax.axis_size("pitch")
    n_span = lax.axis_size("span")
    n_var, n_row, n_col, n_cell = flow.shape
    n_term = lower_coef.shape[0]
    sizes = (n_axial, n_pitch, n_span, n_var, n_row, n_col, n_cell, n_term)
    any_spec = pl.BlockSpec(memory_space=pl.ANY)
    vmem = pl.BlockSpec(memory_space=pltpu.VMEM)
    smem = pl.BlockSpec(memory_space=pltpu.SMEM)
    face = (n_var, n_row, n_cell)
    f32 = jnp.float32
    dma = pltpu.SemaphoreType.DMA
    flow, step, lower_coef, upper_coef, phase_angles, partner, periodic = (
        pltpu.with_memory_space_constraint(a, pltpu.HBM)
        for a in (flow, step, lower_coef, upper_coef, phase_angles, partner, periodic))
    acc, sides = pl.pallas_call(
        functools.partial(kernel, sizes),
        out_shape=(pltpu.VMEM(flow.shape, f32), pltpu.VMEM((2, *face), f32)),
        in_specs=[any_spec] * 4 + [smem] * 3,
        out_specs=(vmem, vmem),
        scratch_shapes=[
            pltpu.VMEM((n_var, n_row + 2, n_col, n_cell), f32),
            pltpu.VMEM(flow.shape, f32),
            pltpu.VMEM((2, n_term, *face), f32),
            pltpu.VMEM((2, *face), f32),
            pltpu.VMEM(face, f32),
            pltpu.VMEM(face, f32),
            pltpu.VMEM(face, f32),
            pltpu.VMEM(face, f32),
            pltpu.VMEM((n_axial, n_var, 1, n_cell), f32),
            pltpu.VMEM((n_axial, n_var, 1, n_cell), f32),
            pltpu.VMEM((2, *face), f32),
            pltpu.VMEM((2, *face), f32),
            pltpu.VMEM((2, n_col, LANES), f32),
            pltpu.VMEM((2, n_col, LANES), f32),
            pltpu.VMEM((2, n_var, n_col, LANES), f32),
            pltpu.VMEM(face, f32),
            pltpu.SMEM((n_axial,), jnp.int32),
            dma((4,)), dma((n_var,)), dma((n_var,)), dma((n_var,)), dma((n_var,)),
            dma((n_var,)), dma((n_var,)), dma, dma, dma((2,)), dma((2,)), dma((2,)), dma((2,)), dma, dma,
            pltpu.SemaphoreType.REGULAR,
        ],
        compiler_params=pltpu.CompilerParams(collective_id=0, has_side_effects=True, vmem_limit_bytes=24 << 20),
        name="section",
    )(flow, step, lower_coef, upper_coef, phase_angles, partner, periodic)
    col = lax.broadcasted_iota(jnp.int32, (1, 1, n_col, 1), 2)
    low, high = sides[0][:, :, None, :], sides[1][:, :, None, :]
    return acc + jnp.where(col == 0, low, jnp.where(col == n_col - 1, high, 0.0))


def solution(mesh):
    in_specs = (
        P(None, "axial", "pitch", "span"),
        P(None, "axial", "pitch", "span"),
        P("pitch", None, "axial", "span"),
        P("pitch", None, "axial", "span"),
        P(None, "axial"),
        P(None, "axial"),
        P(),
    )
    out_specs = P(None, "axial", "pitch", "span")
    return jax.shard_map(
        per_device, mesh=mesh, in_specs=in_specs, out_specs=out_specs, check_vma=False
    )
```

time: 41 us -> 31.7 us (0.77)
  Pallas kernels: 36.8 us -> 30.1 us
  other arithmetic: 4.05 us -> 1.43 us
    pallas_call x1, Pallas kernels: 36.8 us -> 30.1 us  [per_device(): pl.pallas_call(functools.partial(kernel, sizes), out_shape=(pltpu.VMEM(fl...]
    select_n x1 -> x0, other arithmetic: 1.33 us -> none  [term_basis(): jnp.where((term_ids % 2 == 0) & (term_ids > 0), jnp.sin(harmonic * phase_...]
    add x1, other arithmetic: 2.69 us -> 1.43 us  [per_device(): acc + jnp.where(col == 0, low, jnp.where(col == n_col - 1, high, 0.0))]
where the time goes in v2:
time: 31.7 us; the launch traced here: 31.5 us
  Pallas kernels  30.1 us (95%)
  other arithmetic  1.43 us (5%)
    pallas_call x1, Pallas kernels, per_device(): pl.pallas_call(functools.partial(kernel, sizes), out_shape=(pltpu.VMEM(fl...  30.1 us
    add x1, other arithmetic, per_device(): acc + jnp.where(col == 0, low, jnp.where(col == n_col - 1, high, 0.0))  1.43 us

profile of v2, /device:TPU:64, one launch (start us, length us, event | category | flops | bytes accessed | tf_op | source)
XLA Modules:
  0.0 31.5 jit_solution(5446560313894846711)
XLA Ops:
  0.0 30.1 %section.1 = (f32[5,16,8,512]{3,2,1,0:T(8,128)S(1)}, f32[2,5,16,512]{3,2,1,0:T(8,128)S(1)}) custom-call(f32[5,16,8,512]{3,2,1,0:T(8,128)} %flow.1, f32[5,16,8,512]{3,2,1,0:T(8,128)} %step.1, f32[2,5,16,512]{3,2,1,0:T(8,128)} %lower_coef.1, f32[2,5,16,512]{3,2,1,0:T(8,128)} %upper_coef.1, f32[2]{0:T(128)} %phases.1, s32[2,16]{1,0:T(2,128)} %partner.1, ...), custom_call_target="tpu_custom_call" | custom-call | tf_op jit(solution)/shard_map/section/pallas_call | solution.py:454
  30.1 1.4 %select_add_fusion = f32[5,16,8,512]{3,2,1,0:T(8,128)} fusion(f32[5,16,8,512]{3,2,1,0:T(8,128)S(1)} %get-tuple-element.7, f32[5,16,512]{2,1,0:T(8,128)S(1)} %get-tuple-element.10, f32[5,16,512]{2,1,0:T(8,128)S(1)} %get-tuple-element.9, pred[8]{0:T(512)(128)(4,1)S(1)} %get-tuple-element.11, pred[8]{0:T(512)(128)(4,1)S(1)} %get-tuple-element.12), kind=kLoop, calls=%fused_computation | loop fusion | flops 983040 | bytes 2949136 | tf_op jit(solution)/shard_map/add | solution.py:486
  (2 shorter events, 0.0 us)

commit v3 on v2

--- a/solution.py
+++ b/solution.py
@@ -32,17 +32,18 @@
 
 
 def kernel(
-    sizes, flow, step, lower_coef, upper_coef, phases, partner, periodic, out_v, sides,
+    sizes, flow, step, lower_coef, upper_coef, phases_in, partner_in, periodic_in, out_v, sides,
     fx, sx, coef, part, rx_core, rx_near, rx_far, total, slots, recv, edge, halo, span_tx, span_rx, span_in,
-    ghost, table,
+    ghost, phases, partner, periodic, table,
     load_sem, core_send, core_recv, near_send, near_recv, far_send, far_recv, row_send, row_recv,
-    axial_send, axial_recv, pitch_send, pitch_recv, span_send, span_recv, ready,
+    axial_send, axial_recv, pitch_send, pitch_recv, span_send, span_recv, ready, span_ready,
 ):
     n_axial, n_pitch, n_span, n_var, n_row, n_col, n_cell, n_term = sizes
     at = lax.axis_index("axial")
     pitch = lax.axis_index("pitch")
     span = lax.axis_index("span")
     chips = n_pitch // 2
+    n_z = min(n_axial, 8)
     core = lax.rem(pitch, 2)
     chip = lax.div(pitch, 2)
     place = jnp.where(core == 0, chips - 1 - chip, chip)
@@ -71,6 +72,10 @@
 
     load_flow = pltpu.make_async_copy(flow, fx.at[:, pl.ds(1, n_row)], load_sem.at[2])
     load_step = pltpu.make_async_copy(step, sx, load_sem.at[3])
+    load_phases = pltpu.make_async_copy(phases_in, phases, load_sem.at[4])
+    load_partner = pltpu.make_async_copy(partner_in, partner, load_sem.at[5])
+    load_periodic = pltpu.make_async_copy(periodic_in, periodic, load_sem.at[6])
+    load_phases.start()
     @pl.when(core == 0)
     def _():
         load_coef(1).start()
@@ -81,8 +86,8 @@
         load_coef(0).start()
         load_coef(1).start()
 
-    load_flow.start()
-    load_step.start()
+    load_partner.start()
+    load_periodic.start()
 
     barrier = pltpu.get_barrier_semaphore()
 
@@ -91,6 +96,9 @@
 
     one = jnp.int32(1)
     zero = jnp.int32(0)
+
+    def tell(sem, **where):
+        pl.semaphore_signal(sem, inc=1, device_id=where, device_id_type=MESH)
 
     @pl.when(is_end)
     def _():
@@ -98,15 +106,18 @@
         def _(j):
             greet(axial=lax.rem(at + j, n_axial), pitch=helper)
 
-    greetings = jnp.where(is_helper, n_axial - 1, 0)
+    pl.when(is_end)(lambda: greet(pitch=helper))
+    pl.when(is_end)(lambda: greet(pitch=middle))
+    pl.when(is_middle)(lambda: greet(pitch=pitch + 2 * toward))
+    greetings = jnp.where(is_helper, n_axial - 1, zero) + jnp.where(is_end, zero, one)
+    greet(span=1 - span, pitch=jnp.where(span == 1, n_pitch - 3, 2))
+    collector = jnp.where(span == 0, n_pitch - 3, 2)
+    is_collector = pitch == collector
+    pl.when(jnp.logical_not(is_collector))(lambda: greet(pitch=collector))
+    greetings = greetings + jnp.where(is_collector, 2 * n_pitch - 1, zero)
     for holds, where in (
         (None, {"pitch": mate}),
-        (None, {"span": 1 - span}),
         (has_beside, {"pitch": beside}),
-        (pitch >= 2, {"pitch": pitch - 2}),
-        (pitch < n_pitch - 2, {"pitch": pitch + 2}),
-        (is_middle, {"pitch": end}),
-        (is_end, {"pitch": middle}),
         (at > 0, {"axial": at - 1}),
         (at < n_axial - 1, {"axial": at + 1}),
     ):
@@ -117,6 +128,7 @@
             pl.when(holds)(functools.partial(greet, **where))
             greetings = greetings + jnp.where(holds, one, zero)
 
+    load_phases.wait()
     spot = lax.broadcasted_iota(jnp.int32, (8, LANES), 1)
     second = spot >= n_term
     term = pitch * n_term + jnp.where(second, spot - n_term, spot)
@@ -130,8 +142,9 @@
             value = value + first[:1, t : t + 1] * coef[face, t, v]
         part[face, v] = value
 
-    load_coef(0).wait()
-    load_coef(1).wait()
+    pl.when(core == 0)(lambda: load_coef(1).wait())
+    pl.when(core == 1)(lambda: load_coef(0).wait())
+    load_flow.start()
     for v in range(n_var):
         evaluate(1 - core, v)
 
@@ -145,12 +158,33 @@
     for v in range(n_var):
         core_copy(v).start()
 
-    @pl.when(is_helper)
-    def _():
-        pl.semaphore_signal(ready, inc=1, device_id={"pitch": end}, device_id_type=MESH)
-
+    pl.when(is_helper)(lambda: tell(ready, pitch=end))
+
+    @pl.when(is_collector)
+    def _():
+        for k in range(n_pitch):
+            pl.when(pitch != k)(lambda: tell(span_ready, pitch=k))
+
+    load_step.start()
+    pl.when(core == 0)(lambda: load_coef(0).wait())
+    pl.when(core == 1)(lambda: load_coef(1).wait())
     for v in range(n_var):
         evaluate(core, v)
+
+    def near_copy(v):
+        return pltpu.make_async_remote_copy(
+            src_ref=total.at[v], dst_ref=rx_near.at[v], send_sem=near_send.at[v], recv_sem=near_recv.at[v],
+            device_id={"pitch": pitch - 2 * toward}, device_id_type=MESH)
+
+    def far_copy(v):
+        return pltpu.make_async_remote_copy(
+            src_ref=total.at[v], dst_ref=rx_far.at[v], send_sem=far_send.at[v], recv_sem=far_recv.at[v],
+            device_id={"pitch": end}, device_id_type=MESH)
+
+    for v in range(n_var):
+        core_copy(v).wait_recv()
+        total[v] = part[core, v] + rx_core[v]
+        pl.when(is_start | is_helper)(lambda: near_copy(v).start())
 
     load_flow.wait()
 
@@ -204,14 +238,20 @@
         low, high = lax.fori_loop(0, n_row, pack, (blank, blank))
         span_tx[0] = low
         span_tx[1] = high
-        span_copy.start()
         pl.when(core == 0)(lambda: pitch_up().start())
         pl.when(core == 1)(lambda: pitch_down().start())
-        pl.when((core == 0) & (pitch > 0))(lambda: pitch_down().start())
-        pl.when((core == 1) & (pitch < n_pitch - 1))(lambda: pitch_up().start())
-
-    early = is_end | is_middle
-    pl.when(early)(send_edges)
+        pl.when((core == 0) & (pitch > 0) & jnp.logical_not(is_middle))(lambda: pitch_down().start())
+        pl.when((core == 1) & (pitch < n_pitch - 1) & jnp.logical_not(is_middle))(lambda: pitch_up().start())
+
+    def send_span():
+        pl.when(jnp.logical_not(is_collector))(lambda: pl.semaphore_wait(span_ready, 1))
+        span_copy.start()
+
+    send_edges()
+
+
+    load_partner.wait()
+    load_periodic.wait()
 
     @pl.when(is_end)
     def _():
@@ -221,23 +261,6 @@
             for r in range(n_row):
                 index = jnp.where(lax.div(partner[1 - core, r], n_row) == d, r, index)
             table[d] = index
-
-    def near_copy(v):
-        return pltpu.make_async_remote_copy(
-            src_ref=total.at[v], dst_ref=rx_near.at[v], send_sem=near_send.at[v], recv_sem=near_recv.at[v],
-            device_id={"pitch": pitch - 2 * toward}, device_id_type=MESH)
-
-    def far_copy(v):
-        return pltpu.make_async_remote_copy(
-            src_ref=total.at[v], dst_ref=rx_far.at[v], send_sem=far_send.at[v], recv_sem=far_recv.at[v],
-            device_id={"pitch": end}, device_id_type=MESH)
-
-    for v in range(n_var):
-        core_copy(v).wait_recv()
-        total[v] = part[core, v] + rx_core[v]
-        pl.when(is_start | is_helper)(lambda: near_copy(v).start())
-
-    pl.when(jnp.logical_not(early))(send_edges)
 
     if chips > 2:
         @pl.when(is_middle)
@@ -247,6 +270,10 @@
                     near_copy(v).wait_recv()
                     total[v] = total[v] + rx_near[v]
                 far_copy(v).start()
+            pl.when(core == 0)(lambda: pitch_down().start())
+            pl.when(core == 1)(lambda: pitch_up().start())
+
+    send_span()
 
     def row_copy(target):
         return pltpu.make_async_remote_copy(
@@ -273,36 +300,70 @@
 
         pl.semaphore_wait(ready, 1)
 
-        @pl.loop(1, n_axial)
-        def _(j):
-            target = lax.rem(at + j, n_axial)
-            pl.when(jnp.logical_not(is_blade(target)))(lambda: row_copy(target).start())
-            pl.when(is_blade(target) & (span == n_span - 1))(lambda: tip_copy(target).start())
+        order = sorted(range(n_axial), key=lambda d: (first_blade <= d < end_blade, d % n_z))
+        for target in order:
+            if first_blade <= target < end_blade:
+                pl.when((at != target) & (span == n_span - 1))(lambda: tip_copy(target).start())
+            else:
+                pl.when(at != target)(lambda: row_copy(target).start())
 
         own = table[at]
         for v in range(n_var):
             recv[at, v] = total[v, pl.ds(own, 1), :]
 
+    load_step.wait()
+    cell = lax.broadcasted_iota(jnp.int32, (n_col, n_cell), 1)
+    col = lax.broadcasted_iota(jnp.int32, (n_col, n_cell), 0)
+
+    def stencil(i, carry):
+        before = [fx[v, i] for v in range(n_var)]
+        after = [fx[v, i + 2] for v in range(n_var)]
+        flux_before = flux_of(before, pressure_of(before), 1)
+        flux_after = flux_of(after, pressure_of(after), 1)
+        for v in range(n_var):
+            out_v[v, i] = sx[v, i] + 0.125 * (before[v] + after[v]) + 0.25 * (flux_before[v] - flux_after[v])
+        u = [fx[v, i + 1] for v in range(n_var)]
+        p = pressure_of(u)
+        flux = flux_of(u, p, 2)
+        above = as_next(u, flux)
+        below = as_previous(u, flux)
+        for v in range(n_var):
+            down = jnp.where(col == 0, 0.0, pltpu.roll(below[v], 1, 0))
+            up = jnp.where(col == n_col - 1, 0.0, pltpu.roll(above[v], n_col - 1, 0))
+            out_v[v, i] = out_v[v, i] + down + up - 0.75 * u[v]
+        flux = flux_of(u, p, 3)
+        above = as_next(u, flux)
+        below = as_previous(u, flux)
+        for v in range(n_var):
+            down = jnp.where(cell == 0, 0.0, pltpu.roll(below[v], 1, 1))
+            up = jnp.where(cell == n_cell - 1, 0.0, pltpu.roll(above[v], n_cell - 1, 1))
+            out_v[v, i] = out_v[v, i] + down + up
+        return carry
+
+    lax.fori_loop(1, n_row - 1, stencil, 0)
+
+
+    @pl.when(at > 0)
+    def _():
+        axial_up().wait_recv()
+
+    @pl.when(at == 0)
+    def _():
+        for v in range(n_var):
+            fx[v, 0] = fx[v, 1]
+
+    @pl.when(at < n_axial - 1)
+    def _():
+        axial_down().wait_recv()
+
+    @pl.when(at == n_axial - 1)
+    def _():
+        for v in range(n_var):
+            fx[v, n_row + 1] = fx[v, n_row]
+
+    lax.fori_loop(0, 2, lambda k, carry: stencil(k * (n_row - 1), carry), 0)
+
     span_copy.wait_recv()
-
-    @pl.when(at > 0)
-    def _():
-        axial_up().wait_recv()
-
-    @pl.when(at == 0)
-    def _():
-        for v in range(n_var):
-            fx[v, 0] = fx[v, 1]
-
-    @pl.when(at < n_axial - 1)
-    def _():
-        axial_down().wait_recv()
-
-    @pl.when(at == n_axial - 1)
-    def _():
-        for v in range(n_var):
-            fx[v, n_row + 1] = fx[v, n_row]
-
     for side, form in enumerate((as_previous, as_next)):
         u = [span_rx[side]]
         for v in range(1, n_var):
@@ -310,38 +371,16 @@
         for v, value in enumerate(form(u, flux_of(u, pressure_of(u), 3))):
             span_in[side, v] = value
 
-    load_step.wait()
-    cell = lax.broadcasted_iota(jnp.int32, (n_col, n_cell), 1)
-    col = lax.broadcasted_iota(jnp.int32, (n_col, n_cell), 0)
-
-    def stencil(i, carry):
-        before = [fx[v, i] for v in range(n_var)]
-        after = [fx[v, i + 2] for v in range(n_var)]
-        flux_before = flux_of(before, pressure_of(before), 1)
-        flux_after = flux_of(after, pressure_of(after), 1)
-        for v in range(n_var):
-            out_v[v, i] = sx[v, i] + 0.125 * (before[v] + after[v]) + 0.25 * (flux_before[v] - flux_after[v])
-        u = [fx[v, i + 1] for v in range(n_var)]
-        p = pressure_of(u)
-        flux = flux_of(u, p, 2)
-        above = as_next(u, flux)
-        below = as_previous(u, flux)
-        for v in range(n_var):
-            down = jnp.where(col == 0, 0.0, pltpu.roll(below[v], 1, 0))
-            up = jnp.where(col == n_col - 1, 0.0, pltpu.roll(above[v], n_col - 1, 0))
-            out_v[v, i] = out_v[v, i] + down + up - 0.75 * u[v]
-        flux = flux_of(u, p, 3)
-        above = as_next(u, flux)
-        below = as_previous(u, flux)
-        for v in range(n_var):
-            first = pltpu.roll(span_in[0, v], LANES - i, 1)[:, :1]
-            last = pltpu.roll(span_in[1, v], LANES - i, 1)[:, :1]
-            down = jnp.where(cell == 0, first, pltpu.roll(below[v], 1, 1))
-            up = jnp.where(cell == n_cell - 1, last, pltpu.roll(above[v], n_cell - 1, 1))
-            out_v[v, i] = out_v[v, i] + down + up
+    def add_span(i, carry):
+        for v in range(n_var):
+            first = jnp.where(lane == 0, pltpu.roll(span_in[0, v], LANES - i, 1), 0.0)
+            last = jnp.where(lane == LANES - 1, pltpu.roll(span_in[1, v], LANES - 1 - i, 1), 0.0)
+            out_v[v, i, :, pl.ds(0, LANES)] = out_v[v, i, :, pl.ds(0, LANES)] + first
+            out_v[v, i, :, pl.ds(tail, LANES)] = out_v[v, i, :, pl.ds(tail, LANES)] + last
         return carry
 
-    lax.fori_loop(0, n_row, stencil, 0)
+    lax.fori_loop(0, n_row, add_span, 0)
+
 
     def add_side(side, u):
         form = (as_previous, as_next)[side]
@@ -444,7 +483,6 @@
     sizes = (n_axial, n_pitch, n_span, n_var, n_row, n_col, n_cell, n_term)
     any_spec = pl.BlockSpec(memory_space=pl.ANY)
     vmem = pl.BlockSpec(memory_space=pltpu.VMEM)
-    smem = pl.BlockSpec(memory_space=pltpu.SMEM)
     face = (n_var, n_row, n_cell)
     f32 = jnp.float32
     dma = pltpu.SemaphoreType.DMA
@@ -454,7 +492,7 @@
     acc, sides = pl.pallas_call(
         functools.partial(kernel, sizes),
         out_shape=(pltpu.VMEM(flow.shape, f32), pltpu.VMEM((2, *face), f32)),
-        in_specs=[any_spec] * 4 + [smem] * 3,
+        in_specs=[any_spec] * 7,
         out_specs=(vmem, vmem),
         scratch_shapes=[
             pltpu.VMEM((n_var, n_row + 2, n_col, n_cell), f32),
@@ -473,10 +511,13 @@
             pltpu.VMEM((2, n_col, LANES), f32),
             pltpu.VMEM((2, n_var, n_col, LANES), f32),
             pltpu.VMEM(face, f32),
+            pltpu.SMEM(phase_angles.shape, f32),
+            pltpu.SMEM(partner.shape, jnp.int32),
+            pltpu.SMEM(periodic.shape, jnp.int32),
             pltpu.SMEM((n_axial,), jnp.int32),
-            dma((4,)), dma((n_var,)), dma((n_var,)), dma((n_var,)), dma((n_var,)),
+            dma((7,)), dma((n_var,)), dma((n_var,)), dma((n_var,)), dma((n_var,)),
             dma((n_var,)), dma((n_var,)), dma, dma, dma((2,)), dma((2,)), dma((2,)), dma((2,)), dma, dma,
-            pltpu.SemaphoreType.REGULAR,
+            pltpu.SemaphoreType.REGULAR, pltpu.SemaphoreType.REGULAR,
         ],
         compiler_params=pltpu.CompilerParams(collective_id=0, has_side_effects=True, vmem_limit_bytes=24 << 20),
         name="section",

time: 31.7 us -> 29.8 us (0.940)
  Pallas kernels: 30.1 us -> 28.2 us
    pallas_call x1, Pallas kernels: 30.1 us -> 28.2 us  [per_device(): pl.pallas_call(functools.partial(kernel, sizes), out_shape=(pltpu.VMEM(fl...]
where the time goes in v3:
time: 29.8 us; the launch traced here: 29.7 us
  Pallas kernels  28.2 us (95%)
  other arithmetic  1.43 us (5%)
    pallas_call x1, Pallas kernels, per_device(): pl.pallas_call(functools.partial(kernel, sizes), out_shape=(pltpu.VMEM(fl...  28.2 us
    add x1, other arithmetic, per_device(): acc + jnp.where(col == 0, low, jnp.where(col == n_col - 1, high, 0.0))  1.43 us

profile of v3, /device:TPU:64, one launch (start us, length us, event | category | flops | bytes accessed | tf_op | source)
XLA Modules:
  0.0 29.7 jit_solution(7892408817766334804)
XLA Ops:
  0.0 28.2 %section.1 = (f32[5,16,8,512]{3,2,1,0:T(8,128)S(1)}, f32[2,5,16,512]{3,2,1,0:T(8,128)S(1)}) custom-call(f32[5,16,8,512]{3,2,1,0:T(8,128)} %flow.1, f32[5,16,8,512]{3,2,1,0:T(8,128)} %step.1, f32[2,5,16,512]{3,2,1,0:T(8,128)} %lower_coef.1, f32[2,5,16,512]{3,2,1,0:T(8,128)} %upper_coef.1, f32[2]{0:T(128)} %phases_in.1, s32[2,16]{1,0:T(2,128)} %partner_in.1, ...), custom_call_target="tpu_custom_call" | custom-call | tf_op jit(solution)/shard_map/section/pallas_call | solution.py:492
  28.2 1.4 %select_add_fusion = f32[5,16,8,512]{3,2,1,0:T(8,128)} fusion(f32[5,16,8,512]{3,2,1,0:T(8,128)S(1)} %get-tuple-element.7, f32[5,16,512]{2,1,0:T(8,128)S(1)} %get-tuple-element.10, f32[5,16,512]{2,1,0:T(8,128)S(1)} %get-tuple-element.9, pred[8]{0:T(512)(128)(4,1)S(1)} %get-tuple-element.11, pred[8]{0:T(512)(128)(4,1)S(1)} %get-tuple-element.12), kind=kLoop, calls=%fused_computation | loop fusion | flops 983040 | bytes 2949136 | tf_op jit(solution)/shard_map/add | solution.py:527
  (2 shorter events, 0.0 us)

commit v4 on v3

--- a/solution.py
+++ b/solution.py
@@ -34,8 +34,8 @@
 def kernel(
     sizes, flow, step, lower_coef, upper_coef, phases_in, partner_in, periodic_in, out_v, sides,
     fx, sx, coef, part, rx_core, rx_near, rx_far, total, slots, recv, edge, halo, span_tx, span_rx, span_in,
-    ghost, phases, partner, periodic, table,
-    load_sem, core_send, core_recv, near_send, near_recv, far_send, far_recv, row_send, row_recv,
+    ghost, opened, phases, partner, periodic, table,
+    load_sem, coef_sem, core_send, core_recv, near_send, near_recv, far_send, far_recv, row_send, row_recv,
     axial_send, axial_recv, pitch_send, pitch_recv, span_send, span_recv, ready, span_ready,
 ):
     n_axial, n_pitch, n_span, n_var, n_row, n_col, n_cell, n_term = sizes
@@ -64,11 +64,13 @@
     def is_blade(a):
         return (a >= first_blade) & (a < end_blade)
 
-    def load_coef(face):
-        return [
-            pltpu.make_async_copy(upper_coef, coef.at[0], load_sem.at[0]),
-            pltpu.make_async_copy(lower_coef, coef.at[1], load_sem.at[1]),
-        ][face]
+    def load_coef(face, v):
+        source = upper_coef if face == 0 else lower_coef
+        return pltpu.make_async_copy(source.at[:, v], coef.at[face, :, v], coef_sem.at[face, v])
+
+    def wait_coef(mine, v):
+        pl.when(core == 0)(lambda: load_coef(0 if mine else 1, v).wait())
+        pl.when(core == 1)(lambda: load_coef(1 if mine else 0, v).wait())
 
     load_flow = pltpu.make_async_copy(flow, fx.at[:, pl.ds(1, n_row)], load_sem.at[2])
     load_step = pltpu.make_async_copy(step, sx, load_sem.at[3])
@@ -76,15 +78,13 @@
     load_partner = pltpu.make_async_copy(partner_in, partner, load_sem.at[5])
     load_periodic = pltpu.make_async_copy(periodic_in, periodic, load_sem.at[6])
     load_phases.start()
-    @pl.when(core == 0)
-    def _():
-        load_coef(1).start()
-        load_coef(0).start()
-
-    @pl.when(core == 1)
-    def _():
-        load_coef(0).start()
-        load_coef(1).start()
+    for first in range(2):
+
+        @pl.when(core == first)
+        def _():
+            for face in (1 - first, first):
+                for v in range(n_var):
+                    load_coef(face, v).start()
 
     load_partner.start()
     load_periodic.start()
@@ -142,22 +142,18 @@
             value = value + first[:1, t : t + 1] * coef[face, t, v]
         part[face, v] = value
 
-    pl.when(core == 0)(lambda: load_coef(1).wait())
-    pl.when(core == 1)(lambda: load_coef(0).wait())
-    load_flow.start()
-    for v in range(n_var):
-        evaluate(1 - core, v)
-
-    pl.semaphore_wait(barrier, greetings)
-
     def core_copy(v):
         return pltpu.make_async_remote_copy(
             src_ref=part.at[1 - core, v], dst_ref=rx_core.at[v], send_sem=core_send.at[v], recv_sem=core_recv.at[v],
             device_id={"pitch": mate}, device_id_type=MESH)
 
+    pl.semaphore_wait(barrier, greetings)
     for v in range(n_var):
+        wait_coef(False, v)
+        evaluate(1 - core, v)
         core_copy(v).start()
 
+    load_flow.start()
     pl.when(is_helper)(lambda: tell(ready, pitch=end))
 
     @pl.when(is_collector)
@@ -165,11 +161,11 @@
         for k in range(n_pitch):
             pl.when(pitch != k)(lambda: tell(span_ready, pitch=k))
 
+    for v in range(n_var):
+        wait_coef(True, v)
+        evaluate(core, v)
+
     load_step.start()
-    pl.when(core == 0)(lambda: load_coef(0).wait())
-    pl.when(core == 1)(lambda: load_coef(1).wait())
-    for v in range(n_var):
-        evaluate(core, v)
 
     def near_copy(v):
         return pltpu.make_async_remote_copy(
@@ -185,82 +181,6 @@
         core_copy(v).wait_recv()
         total[v] = part[core, v] + rx_core[v]
         pl.when(is_start | is_helper)(lambda: near_copy(v).start())
-
-    load_flow.wait()
-
-    def axial_up():
-        return pltpu.make_async_remote_copy(
-            src_ref=fx.at[:, n_row], dst_ref=fx.at[:, 0], send_sem=axial_send.at[0], recv_sem=axial_recv.at[0],
-            device_id={"axial": at + 1}, device_id_type=MESH)
-
-    def axial_down():
-        return pltpu.make_async_remote_copy(
-            src_ref=fx.at[:, 1], dst_ref=fx.at[:, n_row + 1], send_sem=axial_send.at[1], recv_sem=axial_recv.at[1],
-            device_id={"axial": at - 1}, device_id_type=MESH)
-
-    @pl.when(at < n_axial - 1)
-    def _():
-        axial_up().start()
-
-    @pl.when(at > 0)
-    def _():
-        axial_down().start()
-
-    lane = lax.broadcasted_iota(jnp.int32, (n_col, LANES), 1)
-    span_copy = pltpu.make_async_remote_copy(
-        src_ref=span_tx, dst_ref=span_rx, send_sem=span_send, recv_sem=span_recv,
-        device_id={"span": 1 - span}, device_id_type=MESH)
-
-    def pitch_up():
-        return pltpu.make_async_remote_copy(
-            src_ref=edge.at[1], dst_ref=halo.at[0], send_sem=pitch_send.at[0], recv_sem=pitch_recv.at[0],
-            device_id={"pitch": pitch + 1}, device_id_type=MESH)
-
-    def pitch_down():
-        return pltpu.make_async_remote_copy(
-            src_ref=edge.at[0], dst_ref=halo.at[1], send_sem=pitch_send.at[1], recv_sem=pitch_recv.at[1],
-            device_id={"pitch": pitch - 1}, device_id_type=MESH)
-
-    def pack(i, carry):
-        low, high = carry
-        for v in range(n_var):
-            spot = v * n_row + i
-            last = pltpu.roll(fx[v, i + 1, :, pl.ds(tail, LANES)], spot + 1, 1)
-            first = pltpu.roll(fx[v, i + 1, :, pl.ds(0, LANES)], spot, 1)
-            low = jnp.where(lane == spot, last, low)
-            high = jnp.where(lane == spot, first, high)
-            edge[0, v, pl.ds(i, 1), :] = fx[v, i + 1, pl.ds(0, 1), :]
-            edge[1, v, pl.ds(i, 1), :] = fx[v, i + 1, pl.ds(n_col - 1, 1), :]
-        return low, high
-
-    def send_edges():
-        blank = jnp.ones((n_col, LANES), jnp.float32)
-        low, high = lax.fori_loop(0, n_row, pack, (blank, blank))
-        span_tx[0] = low
-        span_tx[1] = high
-        pl.when(core == 0)(lambda: pitch_up().start())
-        pl.when(core == 1)(lambda: pitch_down().start())
-        pl.when((core == 0) & (pitch > 0) & jnp.logical_not(is_middle))(lambda: pitch_down().start())
-        pl.when((core == 1) & (pitch < n_pitch - 1) & jnp.logical_not(is_middle))(lambda: pitch_up().start())
-
-    def send_span():
-        pl.when(jnp.logical_not(is_collector))(lambda: pl.semaphore_wait(span_ready, 1))
-        span_copy.start()
-
-    send_edges()
-
-
-    load_partner.wait()
-    load_periodic.wait()
-
-    @pl.when(is_end)
-    def _():
-        @pl.loop(0, n_axial)
-        def _(d):
-            index = jnp.int32(0)
-            for r in range(n_row):
-                index = jnp.where(lax.div(partner[1 - core, r], n_row) == d, r, index)
-            table[d] = index
 
     if chips > 2:
         @pl.when(is_middle)
@@ -270,10 +190,89 @@
                     near_copy(v).wait_recv()
                     total[v] = total[v] + rx_near[v]
                 far_copy(v).start()
-            pl.when(core == 0)(lambda: pitch_down().start())
-            pl.when(core == 1)(lambda: pitch_up().start())
-
-    send_span()
+    load_flow.wait()
+
+    def axial_up():
+        return pltpu.make_async_remote_copy(
+            src_ref=fx.at[:, n_row], dst_ref=fx.at[:, 0], send_sem=axial_send.at[0], recv_sem=axial_recv.at[0],
+            device_id={"axial": at + 1}, device_id_type=MESH)
+
+    def axial_down():
+        return pltpu.make_async_remote_copy(
+            src_ref=fx.at[:, 1], dst_ref=fx.at[:, n_row + 1], send_sem=axial_send.at[1], recv_sem=axial_recv.at[1],
+            device_id={"axial": at - 1}, device_id_type=MESH)
+
+    @pl.when(at < n_axial - 1)
+    def _():
+        axial_up().start()
+
+    @pl.when(at > 0)
+    def _():
+        axial_down().start()
+
+    lane = lax.broadcasted_iota(jnp.int32, (n_col, LANES), 1)
+    span_copy = pltpu.make_async_remote_copy(
+        src_ref=span_tx, dst_ref=span_rx, send_sem=span_send, recv_sem=span_recv,
+        device_id={"span": 1 - span}, device_id_type=MESH)
+
+    def pitch_up():
+        return pltpu.make_async_remote_copy(
+            src_ref=edge.at[1], dst_ref=halo.at[0], send_sem=pitch_send.at[0], recv_sem=pitch_recv.at[0],
+            device_id={"pitch": pitch + 1}, device_id_type=MESH)
+
+    def pitch_down():
+        return pltpu.make_async_remote_copy(
+            src_ref=edge.at[0], dst_ref=halo.at[1], send_sem=pitch_send.at[1], recv_sem=pitch_recv.at[1],
+            device_id={"pitch": pitch - 1}, device_id_type=MESH)
+
+    def pack(i, carry):
+        low, high = carry
+        for v in range(n_var):
+            spot = v * n_row + i
+            last = pltpu.roll(fx[v, i + 1, :, pl.ds(tail, LANES)], spot + 1, 1)
+            first = pltpu.roll(fx[v, i + 1, :, pl.ds(0, LANES)], spot, 1)
+            low = jnp.where(lane == spot, last, low)
+            high = jnp.where(lane == spot, first, high)
+        return low, high
+
+    def send_edges():
+        blank = jnp.ones((n_col, LANES), jnp.float32)
+        low, high = lax.fori_loop(0, n_row, pack, (blank, blank))
+        span_tx[0] = low
+        span_tx[1] = high
+        pl.when(is_collector)(lambda: span_copy.start())
+
+        @pl.loop(0, n_row)
+        def _(i):
+            for v in range(n_var):
+                edge[0, v, pl.ds(i, 1), :] = fx[v, i + 1, pl.ds(0, 1), :]
+                edge[1, v, pl.ds(i, 1), :] = fx[v, i + 1, pl.ds(n_col - 1, 1), :]
+
+        pl.when(core == 0)(lambda: pitch_up().start())
+        pl.when(core == 1)(lambda: pitch_down().start())
+        pl.when((core == 0) & (pitch > 0))(lambda: pitch_down().start())
+        pl.when((core == 1) & (pitch < n_pitch - 1))(lambda: pitch_up().start())
+
+    def send_span():
+        pl.semaphore_wait(span_ready, 1)
+        span_copy.start()
+
+    send_edges()
+
+
+    load_partner.wait()
+    load_periodic.wait()
+
+    @pl.when(is_end)
+    def _():
+        @pl.loop(0, n_axial)
+        def _(d):
+            index = jnp.int32(0)
+            for r in range(n_row):
+                index = jnp.where(lax.div(partner[1 - core, r], n_row) == d, r, index)
+            table[d] = index
+
+    pl.when(jnp.logical_not(is_collector))(send_span)
 
     def row_copy(target):
         return pltpu.make_async_remote_copy(
@@ -294,7 +293,7 @@
                 far_copy(v).wait_recv()
                 total[v] = total[v] + rx_far[v]
 
-            @pl.loop(0, n_axial)
+            @pl.loop(0, n_axial, unroll=4)
             def _(d):
                 slots[d, v] = total[v, pl.ds(table[d], 1), :]
 
@@ -400,6 +399,9 @@
     @pl.when(is_end)
     def _():
         blade = is_blade(at)
+        position = lax.broadcasted_iota(jnp.int32, (1, n_cell), 1) + span * n_cell
+        for i in range(n_row):
+            opened[pl.ds(i, 1), :] = jnp.where(position >= n_span * n_cell - periodic[core, i], 1.0, 0.0)
 
         @pl.when(jnp.logical_not(blade))
         def _():
@@ -412,20 +414,18 @@
                 slots.at[pl.ds(0, n_axial - 1), :, :, pl.ds(tail, LANES)],
                 recv.at[pl.ds(0, n_axial - 1), :, :, pl.ds(tail, LANES)], row_recv).wait()
 
-        position = lax.broadcasted_iota(jnp.int32, (1, n_cell), 1) + span * n_cell
-
-        @pl.loop(0, n_row)
-        def _(i):
+        for i in range(n_row):
             source = lax.div(partner[core, i], n_row)
-            is_open = position >= n_span * n_cell - periodic[core, i]
             for v in range(n_var):
-                wall = edge[core, v, pl.ds(i, 1), :]
-                if v == 2:
-                    wall = -wall
-                ghost[v, pl.ds(i, 1), :] = jnp.where(is_open, recv[source, v], wall)
-
-        pl.when(core == 0)(lambda: add_side(0, [ghost[v] for v in range(n_var)]))
-        pl.when(core == 1)(lambda: add_side(1, [ghost[v] for v in range(n_var)]))
+                ghost[v, pl.ds(i, 1), :] = recv[source, v]
+
+        is_open = opened[...] > 0.5
+        u = []
+        for v in range(n_var):
+            wall = edge[core, v]
+            u.append(jnp.where(is_open, ghost[v], -wall if v == 2 else wall))
+        pl.when(core == 0)(lambda: add_side(0, u))
+        pl.when(core == 1)(lambda: add_side(1, u))
 
     for v in range(n_var):
         core_copy(v).wait_send()
@@ -472,6 +472,22 @@
         pitch_down().wait_send()
 
     span_copy.wait_send()
+
+
+def join(acc, sides, out, stage, sem):
+    n_var, n_row, n_col, n_cell = acc.shape
+    col = lax.broadcasted_iota(jnp.int32, (n_col, n_cell), 0)
+
+    def put(v):
+        return pltpu.make_async_copy(stage.at[v], out.at[v], sem.at[v])
+
+    for v in range(n_var):
+        for i in range(n_row):
+            low, high = (jnp.where(col == e, sides[k, v, pl.ds(i, 1), :], 0.0) for k, e in ((0, 0), (1, n_col - 1)))
+            stage[v, i] = acc[v, i] + low + high
+        put(v).start()
+    for v in range(n_var):
+        put(v).wait()
 
 
 def per_device(flow, step, lower_coef, upper_coef, partner, periodic, phase_angles):
@@ -511,20 +527,28 @@
             pltpu.VMEM((2, n_col, LANES), f32),
             pltpu.VMEM((2, n_var, n_col, LANES), f32),
             pltpu.VMEM(face, f32),
+            pltpu.VMEM(face[1:], f32),
             pltpu.SMEM(phase_angles.shape, f32),
             pltpu.SMEM(partner.shape, jnp.int32),
             pltpu.SMEM(periodic.shape, jnp.int32),
             pltpu.SMEM((n_axial,), jnp.int32),
-            dma((7,)), dma((n_var,)), dma((n_var,)), dma((n_var,)), dma((n_var,)),
+            dma((7,)), dma((2, n_var)), dma((n_var,)), dma((n_var,)), dma((n_var,)), dma((n_var,)),
             dma((n_var,)), dma((n_var,)), dma, dma, dma((2,)), dma((2,)), dma((2,)), dma((2,)), dma, dma,
             pltpu.SemaphoreType.REGULAR, pltpu.SemaphoreType.REGULAR,
         ],
         compiler_params=pltpu.CompilerParams(collective_id=0, has_side_effects=True, vmem_limit_bytes=24 << 20),
         name="section",
     )(flow, step, lower_coef, upper_coef, phase_angles, partner, periodic)
-    col = lax.broadcasted_iota(jnp.int32, (1, 1, n_col, 1), 2)
-    low, high = sides[0][:, :, None, :], sides[1][:, :, None, :]
-    return acc + jnp.where(col == 0, low, jnp.where(col == n_col - 1, high, 0.0))
+    acc, sides = (pltpu.with_memory_space_constraint(a, pltpu.VMEM) for a in (acc, sides))
+    return pl.pallas_call(
+        join,
+        out_shape=jax.ShapeDtypeStruct(flow.shape, f32),
+        in_specs=[vmem, vmem],
+        out_specs=any_spec,
+        scratch_shapes=[pltpu.VMEM(flow.shape, f32), dma((n_var,))],
+        compiler_params=pltpu.CompilerParams(vmem_limit_bytes=8 << 20),
+        name="join",
+    )(acc, sides)
 
 
 def solution(mesh):

time: 29.8 us -> 28.5 us (0.956)
  other arithmetic: 1.43 us -> 0 us
    add x1 -> x0, other arithmetic: 1.43 us -> none  [per_device(): acc + jnp.where(col == 0, low, jnp.where(col == n_col - 1, high, 0.0))]
    pallas_call x0 -> x1, Pallas kernels: none -> 1.14 us  [per_device(): pl.pallas_call(join, out_shape=jax.ShapeDtypeStruct(flow.shape, f32), in_...]
    pallas_call x1, Pallas kernels: 28.2 us -> 27.1 us  [per_device(): pl.pallas_call(functools.partial(kernel, sizes), out_shape=(pltpu.VMEM(fl...]
where the time goes in v4:
time: 28.5 us; the launch traced here: 28.3 us
  Pallas kernels  28.3 us (99%)
    pallas_call x1, Pallas kernels, per_device(): pl.pallas_call(functools.partial(kernel, sizes), out_shape=(pltpu.VMEM(fl...  27.1 us
    pallas_call x1, Pallas kernels, per_device(): pl.pallas_call(join, out_shape=jax.ShapeDtypeStruct(flow.shape, f32), in_...  1.14 us

profile of v4, /device:TPU:64, one launch (start us, length us, event | category | flops | bytes accessed | tf_op | source)
XLA Modules:
  0.0 28.3 jit_solution(1209877751908925722)
XLA Ops:
  0.0 27.1 %section.1 = (f32[5,16,8,512]{3,2,1,0:T(8,128)S(1)}, f32[2,5,16,512]{3,2,1,0:T(8,128)S(1)}) custom-call(f32[5,16,8,512]{3,2,1,0:T(8,128)} %flow.1, f32[5,16,8,512]{3,2,1,0:T(8,128)} %step.1, f32[2,5,16,512]{3,2,1,0:T(8,128)} %lower_coef.1, f32[2,5,16,512]{3,2,1,0:T(8,128)} %upper_coef.1, f32[2]{0:T(128)} %phases_in.1, s32[2,16]{1,0:T(2,128)} %partner_in.1, ...), custom_call_target="tpu_custom_call" | custom-call | tf_op jit(solution)/shard_map/section/pallas_call | solution.py:508
  27.1 1.1 %join.1 = f32[5,16,8,512]{3,2,1,0:T(8,128)} custom-call(f32[5,16,8,512]{3,2,1,0:T(8,128)S(1)} %get-tuple-element.7.acc, f32[2,5,16,512]{3,2,1,0:T(8,128)S(1)} %get-tuple-element.8.sides), custom_call_target="tpu_custom_call" | custom-call | tf_op jit(solution)/shard_map/join/pallas_call | solution.py:543
